TPU v7x, 128 devices: a whole 4x4x4 slice. The times are simulated.
128 devices in a mesh: lon: 16 (over x_lo, y, core), lat: 8 (over x_hi, z).
Axes of the slice: x: 4 (x_hi: 2, x_lo: 2; x = x_hi * 2 + x_lo), y: 4, z: 4, core: 2. Of those that a mesh axis runs over, the one named last changes fastest.
Arguments:
- grad_field: float32 [32, 64, 137, 128], P('lat', 'lon'), may hold values from -6 to 6
- lat_weights: float32 [8, 3], replicated, may hold values from 0.2 to 1
- block_offsets: int32 [8, 5], replicated, may hold values from -3 to 3, as said below
- filters: bfloat16 [8, 5, 128, 128], replicated, may hold values from -0.25 to 0.25
- vertical: bfloat16 [8, 137, 137], replicated, may hold values from -0.5 to 0.5
- slot_of_band: int32 [8], replicated, may hold values from 0 to 7, each once
Outputs:
- band_control: bfloat16 [8, 32, 64, 137, 128], P('lat', 'lon')
Inputs may be any that keep to these rules, and one draw needn't show every extreme that they name: `block_offsets`: each band names 5 different offsets; offset -3 is named by some band and offset 3 by some band.
All inputs are finite; a program needn't handle non-finite values.
Results may differ from a plain program's by a relative error of at most 0.0058.
Values may be sent and summed in bfloat16 or wider, within the bound.
A program may use at most 128 MiB of HBM per device.

v0:
```python
import jax
import jax.numpy as jnp
from jax import lax
from jax.sharding import PartitionSpec as P


def extended(value, sides, width):
    for axis, dim in sides:
        count, length = (lax.axis_size(axis), value.shape[dim])
        up = [(i, (i + 1) % count) for i in range(count - 1)]
        down = [(j, i) for i, j in up]
        last = lax.slice_in_dim(value, length - width, length, axis=dim)
        first = lax.slice_in_dim(value, 0, width, axis=dim)
        before = lax.ppermute(last, axis, up)
        after = lax.ppermute(first, axis, down)
        value = jnp.concatenate([before, value, after], axis=dim)
    return value


def slot_tables(lat_weights, block_offsets, filters, vertical, slot_of_band):
    band_count = slot_of_band.shape[0]
    ordinal = jnp.arange(band_count, dtype=jnp.int32)
    matches = (slot_of_band[None, :] == ordinal[:, None]).astype(jnp.int32)
    band_at_slot = jnp.sum(matches * ordinal[None, :], axis=1)
    return tuple(
        (
            jnp.take(source_table, band_at_slot, axis=0)
            for source_table in (lat_weights, block_offsets, filters, vertical)
        )
    )


def blend_rows(framed, weights):
    row_count = framed.shape[0] - 2
    blended = (
        weights[0] * framed[0:row_count]
        + weights[1] * framed[1 : row_count + 1]
        + weights[2] * framed[2 : row_count + 2]
    )
    return blended.astype(jnp.bfloat16)


def band_output(blended, offsets, filter_set, vertical_b, count_q):
    running = None
    for position in range(filter_set.shape[0]):
        picks = (jnp.arange(count_q, dtype=jnp.int32) + offsets[position]) % count_q
        window = jnp.take(blended, picks, axis=1)
        term = jnp.einsum(
            "rqlc,cd->rqld", window, filter_set[position], preferred_element_type=jnp.float32
        )
        running = term if running is None else running + term
    smoothed = running.astype(jnp.bfloat16)
    result = jnp.einsum("ml,rqlc->rqmc", vertical_b, smoothed, preferred_element_type=jnp.float32)
    return result.astype(jnp.bfloat16)


def owned_slots(tables, band_count):
    group = band_count // lax.axis_size("lat")
    first_slot = lax.axis_index("lat") * group
    return (
        group,
        tuple((lax.dynamic_slice_in_dim(table, first_slot, group, 0) for table in tables)),
    )


def on_device(grad_field, lat_weights, block_offsets, filters, vertical, slot_of_band):
    weights_s, offsets_s, filters_s, vertical_s = slot_tables(
        lat_weights, block_offsets, filters, vertical, slot_of_band
    )
    band_count = slot_of_band.shape[0]
    columns = lax.all_gather(grad_field, "lat", axis=0, tiled=True)
    circles = lax.all_to_all(columns, "lon", split_axis=0, concat_axis=1, tiled=True)
    framed = extended(circles, (("lon", 0),), 1)
    group, owned = owned_slots((weights_s, offsets_s, filters_s, vertical_s), band_count)
    weights_g, offsets_g, filters_g, vertical_g = owned
    count_q = circles.shape[1]
    blended = blend_rows(framed, weights_g[0])
    results = [band_output(blended, offsets_g[0], filters_g[0], vertical_g[0], count_q)]
    return jnp.stack(results)


def solution(mesh):
    placed = (P("lat", "lon", None, None), P(), P(), P(), P(), P())
    return jax.shard_map(
        on_device,
        mesh=mesh,
        in_specs=placed,
        out_specs=P("lat", "lon", None, None, None),
        check_vma=False,
    )
```

profile of v0, /device:TPU:2, one launch (start us, length us, event | category | flops | bytes accessed | tf_op | source)
XLA Modules:
  0.0 533.0 jit_solution(3365616534772370330)
XLA Ops:
  6.5 0.7 all-gather.2.cloned.1.call-update
  7.3 116.5 %all-gather.2.cloned.1.call-done = f32[32,4,137,128]{3,1,2,0:T(4,128)} async-done(((f32[4,4,137,128]{3,1,2,0:T(4,128)}), f32[32,4,137,128]{3,1,2,0:T(4,128)}) %all-gather.2.cloned.1.call-update) | async-done | bytes 8978448 | tf_op jit(solution)/shard_map/all_gather | solution.py:71
  123.7 106.2 %all_to_all.18 = f32[32,4,137,128]{3,1,2,0:T(4,128)} all-to-all(f32[32,4,137,128]{3,1,2,0:T(4,128)} %all-gather.2.cloned.1.call-done), channel_id=1, replica_groups=mesh['lon'=16,'lat'=8] {'lon'}, dimensions={0} | all-to-all | bytes 17956864 | tf_op jit(solution)/shard_map/all_to_all | solution.py:72
  229.9 9.7 %copy.80 = f32[16,2,4,137,128]{4,2,0,3,1:T(4,128)} copy(f32[16,2,4,137,128]{4,2,3,1,0:T(4,128)} %bitcast.76) | data formatting | bytes 17956864 | tf_op jit(solution)/shard_map/all_to_all | solution.py:72
  239.6 11.2 %fusion.35 = (f32[1,16,4,137,128]{4,2,1,3,0:T(4,128)}, f32[1,16,4,137,128]{4,2,1,3,0:T(4,128)}) fusion(f32[2,16,4,137,128]{4,2,1,3,0:T(4,128)} %bitcast.74), kind=kLoop, calls=%fused_computation.95 | loop fusion | bytes 17956864 | tf_op jit(solution)/shard_map/slice | solution.py:12
  250.8 9.1 %copy.40 = f32[1,64,137,128]{3,0,2,1:T(1,128)} copy(f32[1,64,137,128]{3,1,2,0:T(8,128)} %bitcast.80) | data formatting | bytes 8978432 | tf_op jit(solution)/shard_map/slice | solution.py:12
  259.8 9.3 %copy.43 = f32[1,64,137,128]{3,0,2,1:T(1,128)} copy(f32[1,64,137,128]{3,1,2,0:T(8,128)} %bitcast.79) | data formatting | bytes 8978432 | tf_op jit(solution)/shard_map/slice | solution.py:13
  269.1 3.7 collective-permute-start.1
  272.9 1.9 collective-permute-start
  274.8 0.1 copy.38
  274.9 0.1 select_reduce_fusion
  275.1 0.6 gather_fusion.1
  275.6 0.6 gather_fusion
  276.2 2.2 gather_fusion.3
  278.4 0.8 gather_fusion.2
  279.2 0.6 dynamic-slice
  279.8 0.1 broadcast_select_fusion.6
  279.9 0.7 fusion.37
  280.6 0.6 compare_and_fusion.4
  281.2 0.6 compare_select_fusion.4
  281.9 0.1 broadcast_select_fusion.7
  281.9 1.3 compare_and_fusion
  283.2 1.3 compare_select_fusion
  284.5 1.3 compare_and_fusion.2
  285.8 1.3 compare_select_fusion.2
  287.1 0.6 fusion.38
  287.7 0.8 broadcast_select_fusion.5
  288.5 0.6 dynamic-slice_select_fusion
  289.1 13.0 %copy.41 = f32[2,64,137,128]{3,0,2,1:T(2,128)S(1)} copy(f32[2,64,137,128]{3,1,2,0:T(8,128)} %bitcast.75) | data formatting | bytes 17956864 | tf_op jit(solution)/shard_map/all_to_all | solution.py:72
  302.1 20.3 %collective-permute-done.1 = f32[1,64,137,128]{3,0,2,1:T(1,128)} collective-permute-done((f32[1,64,137,128]{3,0,2,1:T(1,128)}, f32[1,64,137,128]{3,0,2,1:T(1,128)}, u32[]{:S(2)}, u32[]{:S(2)}) %collective-permute-start.1) | collective-permute-done | bytes 4489248 | tf_op jit(solution)/shard_map/ppermute | solution.py:15
  322.4 5.9 %collective-permute-done = f32[1,64,137,128]{3,0,2,1:T(1,128)} collective-permute-done((f32[1,64,137,128]{3,0,2,1:T(1,128)}, f32[1,64,137,128]{3,0,2,1:T(1,128)}, u32[]{:S(2)}, u32[]{:S(2)}) %collective-permute-start) | collective-permute-done | bytes 4489248 | tf_op jit(solution)/shard_map/ppermute | solution.py:14
  328.3 26.4 %fusion.4 = bf16[2,64,137,128]{3,0,2,1:T(2,128)(2,1)} fusion(f32[1,64,137,128]{3,0,2,1:T(1,128)} %collective-permute-done.1, f32[2,64,137,128]{3,0,2,1:T(2,128)S(1)} %copy.41, f32[1,64,137,128]{3,0,2,1:T(1,128)} %collective-permute-done, f32[]{:T(128)} %bitcast.10, f32[]{:T(128)} %bitcast.8, f32[]{:T(128)} %bitcast.3), kind=kLoop, calls=%fused_computation.21 | loop fusion | flops 17956864 | bytes 22446092 | tf_op jit(solution)/shard_map/convert_element_type | solution.py:40
  354.7 13.7 %gather_fusion.8 = bf16[64,2,137,128]{3,1,2,0:T(2,128)(2,1)} fusion(bf16[2,64,137,128]{3,0,2,1:T(2,128)(2,1)} %fusion.4, s32[1024]{0:T(1024)S(1)} %pad_clamp_fusion), kind=kCustom, calls=%fused_computation.4.clone | custom fusion | bytes 8978688 | tf_op jit(solution)/shard_map/jit(_take)/gather | solution.py:47
  368.3 13.7 %gather_fusion.7 = bf16[64,2,137,128]{3,1,2,0:T(2,128)(2,1)} fusion(bf16[2,64,137,128]{3,0,2,1:T(2,128)(2,1)} %fusion.4, s32[1024]{0:T(1024)S(1)} %pad_clamp_fusion.1), kind=kCustom, calls=%fused_computation.3.clone | custom fusion | bytes 8978688 | tf_op jit(solution)/shard_map/jit(_take)/gather | solution.py:47
  382.0 13.6 %gather_fusion.6 = bf16[64,2,137,128]{3,1,2,0:T(2,128)(2,1)} fusion(bf16[2,64,137,128]{3,0,2,1:T(2,128)(2,1)} %fusion.4, s32[1024]{0:T(1024)S(1)} %pad_clamp_fusion.2), kind=kCustom, calls=%fused_computation.2.clone | custom fusion | bytes 8978688 | tf_op jit(solution)/shard_map/jit(_take)/gather | solution.py:47
  395.6 24.6 %gather_fusion.5 = bf16[64,2,137,128]{3,1,2,0:T(2,128)(2,1)} fusion(bf16[2,64,137,128]{3,0,2,1:T(2,128)(2,1)} %fusion.4, s32[1024]{0:T(1024)S(1)} %pad_clamp_fusion.3), kind=kCustom, calls=%fused_computation.1.clone | custom fusion | bytes 8978688 | tf_op jit(solution)/shard_map/jit(_take)/gather | solution.py:47
  420.3 13.7 %gather_fusion.4 = bf16[64,2,137,128]{3,1,2,0:T(2,128)(2,1)} fusion(bf16[2,64,137,128]{3,0,2,1:T(2,128)(2,1)} %fusion.4, s32[1024]{0:T(1024)S(1)} %pad_clamp_fusion.4), kind=kCustom, calls=%fused_computation.clone | custom fusion | bytes 8978688 | tf_op jit(solution)/shard_map/jit(_take)/gather | solution.py:47
  434.0 8.4 %fusion.18 = bf16[2,64,137,128]{3,0,2,1:T(2,128)(2,1)} fusion(bf16[64,2,137,128]{3,1,2,0:T(2,128)(2,1)} %gather_fusion.6, pred[64]{0:T(512)(128)(4,1)S(1)} %get-tuple-element.24), kind=kLoop, calls=%fused_computation.36 | loop fusion | flops 2244608 | bytes 8978496 | tf_op jit(solution)/shard_map/jit(_take)/select_n | solution.py:47
  442.4 8.5 %fusion.17 = bf16[2,64,137,128]{3,0,2,1:T(2,128)(2,1)} fusion(bf16[64,2,137,128]{3,1,2,0:T(2,128)(2,1)} %gather_fusion.5, pred[64]{0:T(512)(128)(4,1)S(1)} %get-tuple-element.25), kind=kLoop, calls=%fused_computation.35 | loop fusion | flops 2244608 | bytes 8978496 | tf_op jit(solution)/shard_map/jit(_take)/select_n | solution.py:47
  450.8 7.4 %fusion.12 = f32[2,64,137,128]{3,2,1,0:T(8,128)} fusion(bf16[2,64,137,128]{3,0,2,1:T(2,128)(2,1)} %fusion.17, bf16[1,5,128,128]{3,2,1,0:T(8,128)(2,1)S(1)} %dynamic-slice_select_fusion), kind=kOutput, calls=%fused_computation.29 | convolution fusion | flops 574619648 | bytes 13500416 | tf_op jit(solution)/shard_map/rqlc,cd->rqld/dot_general | solution.py:48
  458.3 4.6 fusion.10
  462.9 8.4 %fusion.19 = bf16[2,64,137,128]{3,0,2,1:T(2,128)(2,1)} fusion(bf16[64,2,137,128]{3,1,2,0:T(2,128)(2,1)} %gather_fusion.7, pred[64]{0:T(512)(128)(4,1)S(1)} %get-tuple-element.23), kind=kLoop, calls=%fused_computation.37 | loop fusion | flops 2244608 | bytes 8978496 | tf_op jit(solution)/shard_map/jit(_take)/select_n | solution.py:47
  471.3 7.3 %fusion.8 = f32[2,64,137,128]{3,2,1,0:T(8,128)} fusion(bf16[2,64,137,128]{3,0,2,1:T(2,128)(2,1)} %fusion.19, bf16[1,5,128,128]{3,2,1,0:T(8,128)(2,1)S(1)} %dynamic-slice_select_fusion), kind=kOutput, calls=%fused_computation.25 | convolution fusion | flops 574619648 | bytes 13500416 | tf_op jit(solution)/shard_map/rqlc,cd->rqld/dot_general | solution.py:48
  478.7 8.4 %fusion.20 = bf16[2,64,137,128]{3,0,2,1:T(2,128)(2,1)} fusion(bf16[64,2,137,128]{3,1,2,0:T(2,128)(2,1)} %gather_fusion.8, pred[64]{0:T(512)(128)(4,1)S(1)} %get-tuple-element.22), kind=kLoop, calls=%fused_computation.38 | loop fusion | flops 2244608 | bytes 8978496 | tf_op jit(solution)/shard_map/jit(_take)/select_n | solution.py:47
  487.1 7.3 %fusion.6 = f32[2,64,137,128]{3,2,1,0:T(8,128)} fusion(bf16[2,64,137,128]{3,0,2,1:T(2,128)(2,1)} %fusion.20, bf16[1,5,128,128]{3,2,1,0:T(8,128)(2,1)S(1)} %dynamic-slice_select_fusion), kind=kOutput, calls=%fused_computation.23 | convolution fusion | flops 574619648 | bytes 13500416 | tf_op jit(solution)/shard_map/rqlc,cd->rqld/dot_general | solution.py:48
  494.4 8.6 %fusion.16 = bf16[2,64,137,128]{3,0,2,1:T(2,128)(2,1)} fusion(bf16[64,2,137,128]{3,1,2,0:T(2,128)(2,1)} %gather_fusion.4, pred[64]{0:T(512)(128)(4,1)S(1)} %compare_and_fusion.4), kind=kLoop, calls=%fused_computation.34 | loop fusion | flops 2244608 | bytes 8978496 | tf_op jit(solution)/shard_map/jit(_take)/select_n | solution.py:47
  503.0 17.1 %convert_bitcast_fusion = bf16[1,2,64,137,128]{4,3,2,1,0:T(8,128)(2,1)} fusion(f32[2,64,137,128]{3,2,1,0:T(8,128)} %fusion.6, f32[2,64,137,128]{3,2,1,0:T(8,128)} %fusion.8, f32[2,64,137,128]{3,2,1,0:T(8,128)} %fusion.10, f32[2,64,137,128]{3,2,1,0:T(8,128)} %fusion.12, bf16[2,64,137,128]{3,0,2,1:T(2,128)(2,1)} %fusion.16, ...), kind=kOutput, calls=%fused_computation.33 | convolution fusion | flops 1203109888 | bytes 45065216 | tf_op jit(solution)/shard_map/ml,rqlc->rqmc/dot_general | solution.py:53
  520.1 5.6 %copy.50 = bf16[1,2,64,137,128]{4,2,3,1,0:T(8,128)(2,1)} copy(bf16[1,2,64,137,128]{4,3,2,1,0:T(8,128)(2,1)} %convert_bitcast_fusion) | data formatting | bytes 8978432 | tf_op jit(solution)/shard_map/stack | solution.py:79
  (28 shorter events, 0.1 us)
Async XLA Ops:
  6.5 271.8 %copy-start = (bf16[8,5,128,128]{3,2,1,0:T(8,128)(2,1)S(1)}, bf16[8,5,128,128]{3,2,1,0:T(8,128)(2,1)}, u32[]{:S(2)}) copy-start(bf16[8,5,128,128]{3,2,1,0:T(8,128)(2,1)} %param.11) | copy-start | bytes 3932164
  6.5 117.2 %all-gather.2.cloned.1.call-start = ((), (), s32[]{:S(2)}) async-start(), calls=%async_computation.1 | async-start | bytes 10100736 | tf_op jit(solution)/shard_map/all_gather | solution.py:71
  259.8 15.0 %copy-start.4 = (f32[8,3]{0,1:T(4,128)S(1)}, f32[8,3]{0,1:T(4,128)}, u32[]{:S(2)}) copy-start(f32[8,3]{0,1:T(4,128)} %param.9) | copy-start | bytes 292
  259.8 15.1 %copy-start.5 = (s32[8]{0:T(128)S(1)}, s32[8]{0:T(128)}, u32[]{:S(2)}) copy-start(s32[8]{0:T(128)} %param.13) | copy-start | bytes 100
  259.8 15.2 %copy-start.3 = (s32[8,5]{1,0:T(8,128)S(1)}, s32[8,5]{1,0:T(8,128)}, u32[]{:S(2)}) copy-start(s32[8,5]{1,0:T(8,128)} %param.10) | copy-start | bytes 484
  259.8 16.4 %copy-start.2 = (bf16[8,137,137]{2,0,1:T(8,128)(2,1)S(1)}, bf16[8,137,137]{2,0,1:T(8,128)(2,1)}, u32[]{:S(2)}) copy-start(bf16[8,137,137]{2,0,1:T(8,128)(2,1)} %param.12) | copy-start | bytes 900916
  269.1 53.2 %collective-permute-start.1 = (f32[1,64,137,128]{3,0,2,1:T(1,128)}, f32[1,64,137,128]{3,0,2,1:T(1,128)}, u32[]{:S(2)}, u32[]{:S(2)}) collective-permute-start(f32[1,64,137,128]{3,0,2,1:T(1,128)} %copy.43), channel_id=1, source_target_pairs={{8,0},{16,8},{24,16},{32,24},{40,32},{48,40},{56,48},{64,56},{72,6... | collective-permute-start | bytes 13467656 | tf_op jit(solution)/shard_map/ppermute | solution.py:15
  272.9 55.4 %collective-permute-start = (f32[1,64,137,128]{3,0,2,1:T(1,128)}, f32[1,64,137,128]{3,0,2,1:T(1,128)}, u32[]{:S(2)}, u32[]{:S(2)}) collective-permute-start(f32[1,64,137,128]{3,0,2,1:T(1,128)} %copy.40), channel_id=1, source_target_pairs={{0,8},{8,16},{16,24},{24,32},{32,40},{40,48},{48,56},{56,64},{64,7... | collective-permute-start | bytes 13467656 | tf_op jit(solution)/shard_map/ppermute | solution.py:14
  442.4 15.9 %slice-start = ((s8[4489216]{0:T(1024)(128)(4,1)}), s8[294912]{0:T(1024)(128)(4,1)S(1)}, s32[]{:S(2)}) async-start(s8[4489216]{0:T(1024)(128)(4,1)} %bitcast.77), calls=%async_computation.2 | async-start | bytes 589824
  450.8 7.5 %slice-start.1 = ((s8[4489216]{0:T(1024)(128)(4,1)}), s8[4194304]{0:T(1024)(128)(4,1)S(1)}, s32[]{:S(2)}) async-start(s8[4489216]{0:T(1024)(128)(4,1)} %bitcast.77), calls=%async_computation.3 | async-start | bytes 8388608
  503.0 22.7 %copy-start.1 = (bf16[8,5,128,128]{3,2,1,0:T(8,128)(2,1)S(1)}, bf16[8,5,128,128]{3,2,1,0:T(8,128)(2,1)}, u32[]{:S(2)}) copy-start(bf16[8,5,128,128]{3,2,1,0:T(8,128)(2,1)} %param.11) | copy-start | bytes 3932164
Sparse Core Ops, SparseCore 0:
  9.7 114.0 all-gather.1
where the time goes:
time: 543 us; the launch traced here: 533 us
  local copies, waits for them, and re-layouts  143 us (26%)
  waiting for transfers between devices  143 us (26%)
  blocking collectives  106 us (20%)
  other arithmetic  76.7 us (14%)
  matrix products  43.8 us (8%)
  between operations  14 us (3%)
  starting transfers between devices  5.67 us (1%)
    all_gather x1, waiting for transfers between devices, on_device(): columns = lax.all_gather(grad_field, 'lat', axis=0, tiled=True)  116 us
    all_to_all x1, blocking collectives, on_device(): lax.all_to_all(columns, 'lon', split_axis=0, concat_axis=1, tiled=True)  106 us
    gather x5, local copies, waits for them, and re-layouts, band_output(): window = jnp.take(blended, picks, axis=1)  79.3 us
    select_n x8, other arithmetic, band_output(): window = jnp.take(blended, picks, axis=1)  45.4 us
    dot_general x4, matrix products, band_output(): jnp.einsum('rqlc,cd->rqld', window, filter_set[position], preferred_eleme...  26.8 us
    convert_element_type x1, other arithmetic, blend_rows(): return blended.astype(jnp.bfloat16)  26.4 us
    all_to_all x2, local copies, waits for them, and re-layouts, on_device(): lax.all_to_all(columns, 'lon', split_axis=0, concat_axis=1, tiled=True)  22.6 us
    ppermute x1, waiting for transfers between devices, extended(): after = lax.ppermute(first, axis, down)  20.3 us
  transfers between devices with their start and end apart: 3, of which 3 were waited for; matrix products, arithmetic and copies ran while one was open for 5% of the time, Pallas kernels for 0%

commit v1 on v0

v1 whole, which is shorter than its diff:
```python
import functools

import jax
import jax.numpy as jnp
from jax import lax
from jax.experimental import pallas as pl
from jax.experimental.pallas import tpu as pltpu
from jax.sharding import PartitionSpec as P

MESH = pl.DeviceIdType.MESH
SPLIT = 1
LATE = 0


def gather_kernel(levels, pad, x_ref, f_ref, staged, blank, send_sems, first_sems, recv_sems, halo_send, halo_recv, fill_sem):
    o, t = lax.axis_index("lon"), lax.axis_index("lat")
    xh, z = t // 4, t % 4
    zp, zm = xh * 4 + (z + 1) % 4, xh * 4 + (z + 3) % 4
    xp = (1 - xh) * 4 + z
    owner_lat, core = o // 2, o % 2
    nq = 4 // SPLIT
    per = 2 * SPLIT

    barrier = pltpu.get_barrier_semaphore()

    def greet(lon, lat):
        pl.semaphore_signal(barrier, inc=1, device_id={"lon": lon, "lat": lat}, device_id_type=MESH)

    for k in range(2):
        greet(2 * t + k, owner_lat)
    for lat in (zp, zm, xp):
        greet(o, lat)

    @pl.when(o > 0)
    def _():
        greet(o - 1, t)

    @pl.when(o < 15)
    def _():
        greet(o + 1, t)

    def stage(k):
        for i in (2 * k, 2 * k + 1):
            for q in range(4):
                value = x_ref[pl.ds(i * levels * 4 + q, levels, stride=4), :]
                staged[i, q, 0:levels, :] = value.astype(jnp.bfloat16)
                staged[i, q, levels:pad, :] = jnp.zeros((pad - levels, 128), jnp.bfloat16)

    stage(0)
    edge = (o == 0).astype(jnp.int32) + (o == 15).astype(jnp.int32)
    pl.semaphore_wait(barrier, 7 - edge)

    def first(k, s):
        src = staged.at[pl.ds(2 * k, 2), pl.ds(s * nq, nq)]
        dst = f_ref.at[pl.ds(1, 2), pl.ds(4 * o + s * nq, nq)]
        far = pltpu.make_async_remote_copy(
            src, dst, first_sems.at[k, s], recv_sems.at[0, 0, core * SPLIT + s],
            device_id={"lon": 2 * t + k, "lat": owner_lat}, device_id_type=MESH,
        )
        near = pltpu.make_async_copy(src, dst, recv_sems.at[0, 0, core * SPLIT + s])
        mine = (owner_lat == t) & (core == k)
        return far, near, mine

    def start_first(k):
        for s in range(SPLIT):
            far, near, mine = first(k, s)

            @pl.when(mine)
            def _():
                near.start()

            @pl.when(jnp.logical_not(mine))
            def _():
                far.start()

    start_first(0)
    stage(1)
    start_first(1)

    @pl.when(edge > 0)
    def _():
        blank[...] = jnp.zeros_like(blank)
        row = jnp.where(o == 0, 0, 3)
        fills = [pltpu.make_async_copy(blank, f_ref.at[row, pl.ds(c * 8, 8)], fill_sem.at[c]) for c in range(8)]
        for f in fills:
            f.start()
        for f in fills:
            f.wait()

    sends = []

    def rows_of(dx, dz, j):
        owner = ((xh + dx) % 2) * 4 + (z + dz) % 4
        return pl.ds(owner * 8 + j * nq, nq)

    def piece(dx, dz, j):
        return f_ref.at[pl.ds(1, 2), rows_of(dx, dz, j)]

    def send(dx, dz, j, to, there):
        ref = piece(dx, dz, j)
        copy = pltpu.make_async_remote_copy(
            ref, ref, send_sems.at[len(sends)], recv_sems.at[there[0], there[1], j],
            device_id={"lon": o, "lat": to}, device_id_type=MESH,
        )
        copy.start()
        sends.append(copy)

    def halo(dx, dz, j, side):
        q = rows_of(dx, dz, j)
        src = f_ref.at[1 + side, q]
        dst = f_ref.at[3 - 3 * side, q]
        slot = (dx * 4 + dz) * per + j
        return pltpu.make_async_remote_copy(
            src, dst, halo_send.at[side, slot], halo_recv.at[side, slot],
            device_id={"lon": o - 1 + 2 * side, "lat": t}, device_id_type=MESH,
        )

    def each_halo(action):
        @pl.when(o > 0)
        def _():
            action(0)

        @pl.when(o < 15)
        def _():
            action(1)

    def arrive(dx, dz, j):
        ref = piece(dx, dz, j)
        pltpu.make_async_copy(ref, ref, recv_sems.at[dx, dz, j]).wait()
        late = j >= per - LATE
        ring = dx == 0 or not late
        if dx == 0 and (dz == 0 or late):
            if dz == 0:
                send(dx, dz, j, xp, (1, 0))
        if ring and dz == 0:
            send(dx, dz, j, zp, (dx, 3))
            send(dx, dz, j, zm, (dx, 1))
        if ring and dz == 3 and j < per // 2:
            send(dx, dz, j, zp, (dx, 2))
        if ring and dz == 1 and j >= per // 2:
            send(dx, dz, j, zm, (dx, 2))
        if dx == 0 and dz != 0 and late:
            send(dx, dz, j, xp, (1, dz))
        each_halo(lambda side: halo(dx, dz, j, side).start())

    order = [(0, 0), (0, 1), (0, 3), (1, 0), (0, 2), (1, 1), (1, 3), (1, 2)]
    for dx, dz in order:
        for j in range(per):
            arrive(dx, dz, j)

    for k in range(2):
        for s in range(SPLIT):
            far, near, mine = first(k, s)

            @pl.when(jnp.logical_not(mine))
            def _():
                far.wait_send()
    for copy in sends:
        copy.wait_send()
    for dx, dz in order:
        for j in range(per):
            each_halo(lambda side: halo(dx, dz, j, side).wait_send())

            @pl.when(o < 15)
            def _():
                halo(dx, dz, j, 0).wait_recv()

            @pl.when(o > 0)
            def _():
                halo(dx, dz, j, 1).wait_recv()


def gather_rows(x, levels, pad):
    per = 2 * SPLIT
    n_sends = 64 * SPLIT
    return pl.pallas_call(
        functools.partial(gather_kernel, levels, pad),
        out_shape=jax.ShapeDtypeStruct((4, 64, pad, 128), jnp.bfloat16),
        in_specs=[pl.BlockSpec(memory_space=pltpu.VMEM)],
        out_specs=pl.BlockSpec(memory_space=pl.ANY),
        scratch_shapes=[
            pltpu.VMEM((4, 4, pad, 128), jnp.bfloat16),
            pltpu.VMEM((8, pad, 128), jnp.bfloat16),
            pltpu.SemaphoreType.DMA((n_sends,)),
            pltpu.SemaphoreType.DMA((2, SPLIT)),
            pltpu.SemaphoreType.DMA((2, 4, per)),
            pltpu.SemaphoreType.DMA((2, 8 * per)),
            pltpu.SemaphoreType.DMA((2, 8 * per)),
            pltpu.SemaphoreType.DMA((8,)),
        ],
        compiler_params=pltpu.CompilerParams(
            collective_id=0, has_side_effects=True, vmem_limit_bytes=40 << 20
        ),
        cost_estimate=pl.CostEstimate(flops=0, bytes_accessed=20 << 20, transcendentals=0),
        name="gather_rows",
    )(x)


def band_kernel(levels, pad, weights_ref, offsets_ref, slots_ref, f_ref, filters_ref, vertical_ref, out_ref, blended, taps, vert, mixed):
    step = pl.program_id(0)
    me = lax.axis_index("lat")
    band = jnp.int32(0)
    for b in range(8):
        band = band + jnp.where(slots_ref[b] == me, b, 0)

    @pl.when(step == 0)
    def _():
        taps[...] = jnp.zeros_like(taps)
        for tap in range(-3, 4):
            total = jnp.zeros((128, 128), jnp.float32)
            for k in range(5):
                hit = (offsets_ref[band, k] == tap).astype(jnp.float32)
                total = total + hit * filters_ref[band, k].astype(jnp.float32)
            block = total.astype(jnp.bfloat16)
            for m in range(2):
                at = tap + 3 + m
                taps[at * 128 : (at + 1) * 128, m * 128 : (m + 1) * 128] = block
        chosen = lax.broadcasted_iota(jnp.int32, (levels, 8, levels), 1) == band
        picked = jnp.sum(jnp.where(chosen, vertical_ref[...].astype(jnp.float32), 0.0), axis=1)
        vert[...] = jnp.zeros_like(vert)
        vert[0:levels, 0:levels] = picked.astype(jnp.bfloat16)

    w0, w1, w2 = weights_ref[0, band], weights_ref[1, band], weights_ref[2, band]
    chunk = (step + 7) % 8

    def blend(q, carry):
        rows = [f_ref[i, q].astype(jnp.float32) for i in range(4)]
        for i in range(2):
            value = w0 * rows[i] + w1 * rows[i + 1] + w2 * rows[i + 2]
            blended[i, chunk * 8 + q] = value.astype(jnp.bfloat16)
        return carry

    lax.fori_loop(0, 8, blend, 0)

    @pl.when(step >= 2)
    def _():
        base = (step - 2) * 8
        for i in range(2):
            def pair(p, carry):
                q = base + 2 * p
                parts = [blended[i, (q + 61 + n) % 64] for n in range(8)]
                lhs = jnp.concatenate(parts, axis=1)
                smooth = jnp.dot(lhs, taps[...], preferred_element_type=jnp.float32).astype(jnp.bfloat16)
                result = jnp.dot(vert[...], smooth, preferred_element_type=jnp.float32)
                for m in range(2):
                    mixed[pl.ds(2 * p + m, pad, stride=8), :] = result[:, m * 128 : (m + 1) * 128]
                return carry

            lax.fori_loop(0, 4, pair, 0)
            flat = mixed[0 : levels * 8, :].astype(jnp.bfloat16)
            out_ref[i] = flat.reshape(levels, 8, 128)


def band_output(weights, offsets, slots, rows, filters, vertical, levels, pad):
    whole = lambda *shape: pl.BlockSpec(shape, lambda s, *_: (0,) * len(shape), pipeline_mode=pl.Buffered(1))
    return pl.pallas_call(
        functools.partial(band_kernel, levels, pad),
        out_shape=jax.ShapeDtypeStruct((2, levels, 64, 128), jnp.bfloat16),
        grid_spec=pltpu.PrefetchScalarGridSpec(
            num_scalar_prefetch=3,
            grid=(10,),
            in_specs=[
                pl.BlockSpec((4, 8, pad, 128), lambda s, *_: (0, (s + 7) % 8, 0, 0)),
                whole(8, 5, 128, 128),
                whole(levels, 8, levels),
            ],
            out_specs=pl.BlockSpec((2, levels, 8, 128), lambda s, *_: (0, 0, jnp.maximum(s - 2, 0), 0)),
            scratch_shapes=[
                pltpu.VMEM((2, 64, pad, 128), jnp.bfloat16),
                pltpu.VMEM((1024, 256), jnp.bfloat16),
                pltpu.VMEM((pad, pad), jnp.bfloat16),
                pltpu.VMEM((pad * 8, 128), jnp.float32),
            ],
        ),
        compiler_params=pltpu.CompilerParams(vmem_limit_bytes=48 << 20),
        name="band_output",
    )(weights, offsets, slots, rows, filters, vertical)


def on_device(grad_field, lat_weights, block_offsets, filters, vertical, slot_of_band):
    levels = grad_field.shape[2]
    pad = (levels + 15) // 16 * 16
    x = grad_field.transpose(0, 2, 1, 3).reshape(-1, 128)
    rows = gather_rows(x, levels, pad)
    out = band_output(
        lat_weights.T, block_offsets, slot_of_band, rows, filters, vertical.transpose(1, 0, 2), levels, pad
    )
    return out.transpose(0, 2, 1, 3)[None]


def solution(mesh):
    placed = (P("lat", "lon", None, None), P(), P(), P(), P(), P())
    return jax.shard_map(
        on_device,
        mesh=mesh,
        in_specs=placed,
        out_specs=P("lat", "lon", None, None, None),
        check_vma=False,
    )
```

time: 543 us -> 125 us (0.23)
  the two profiles are of different devices: /device:TPU:2 before, /device:TPU:38 now
where the time goes in v1:
time: 125 us
  Pallas kernels  120 us (96%)
  local copies, waits for them, and re-layouts  4.89 us (4%)
    pallas_call x1, Pallas kernels, gather_rows(): pl.pallas_call(functools.partial(gather_kernel, levels, pad), out_shape=j...  83 us
    pallas_call x1, Pallas kernels, band_output(): pl.pallas_call(functools.partial(band_kernel, levels, pad), out_shape=jax...  36.6 us
    unnamed x14, local copies, waits for them, and re-layouts  4.89 us

profile of v1, /device:TPU:38, one launch (start us, length us, event | category | flops | bytes accessed | tf_op | source)
XLA Modules:
  0.0 124.6 jit_solution(155705802527172161)
XLA Ops:
  0.0 0.0 copy-start.2
  0.0 1.2 %copy-done.2 = f32[4,4,137,128]{3,1,2,0:T(4,128)S(1)} copy-done((f32[4,4,137,128]{3,1,2,0:T(4,128)S(1)}, f32[4,4,137,128]{3,1,2,0:T(4,128)}, u32[]{:S(2)}) %copy-start.2) | copy-done | bytes 1122328
  1.3 0.0 copy-start.1
  1.3 0.0 copy-start.3
  1.3 0.0 copy-start.4
  1.3 0.0 copy-start.5
  1.3 0.0 copy-start.6
  1.3 83.0 %gather_rows.1.f_ref = bf16[4,64,144,128]{3,2,1,0:T(8,128)(2,1)S(1)} custom-call(f32[2192,128]{1,0:T(8,128)S(1)} %bitcast.8), custom_call_target="tpu_custom_call" | custom-call | bytes 20971520 | tf_op jit(solution)/shard_map/gather_rows/pallas_call | solution.py:176
  84.3 0.0 copy-start
  84.3 3.6 %copy-done = bf16[4,64,144,128]{3,2,1,0:T(8,128)(2,1)} copy-done((bf16[4,64,144,128]{3,2,1,0:T(8,128)(2,1)}, bf16[4,64,144,128]{3,2,1,0:T(8,128)(2,1)S(1)}, u32[]{:S(2)}) %copy-start) | copy-done | bytes 9437208
  87.9 0.0 copy-done.1
  87.9 0.0 copy-done.3
  87.9 0.0 copy-done.4
  87.9 0.0 copy-done.5
  87.9 0.0 copy-done.6
  87.9 36.6 %band_output.1 = bf16[2,137,64,128]{3,2,1,0:T(8,128)(2,1)} custom-call(f32[3,8]{1,0:T(4,128)S(1)} %bitcast.10, s32[8,5]{1,0:T(8,128)S(1)} %copy-done.4, s32[8]{0:T(128)S(1)} %copy-done.6, bf16[4,64,144,128]{3,2,1,0:T(8,128)(2,1)} %copy-done, bf16[8,5,128,128]{3,2,1,0:T(8,128)(2,1)S(1)} %copy-done.1, bf16[137,8,137]{2,1,0:T(8,128)(2,1)S(1)} %bitcast.9), custom_call_target="tpu_custom_call" | custom-call | tf_op jit(solution)/shard_map/band_output/pallas_call | solution.py:256
Async XLA Ops:
  0.0 1.3 %copy-start.2 = (f32[4,4,137,128]{3,1,2,0:T(4,128)S(1)}, f32[4,4,137,128]{3,1,2,0:T(4,128)}, u32[]{:S(2)}) copy-start(f32[4,4,137,128]{3,1,2,0:T(4,128)} %param.6) | copy-start | bytes 3366916
  1.3 86.7 %copy-start.1 = (bf16[8,5,128,128]{3,2,1,0:T(8,128)(2,1)S(1)}, bf16[8,5,128,128]{3,2,1,0:T(8,128)(2,1)}, u32[]{:S(2)}) copy-start(bf16[8,5,128,128]{3,2,1,0:T(8,128)(2,1)} %filters_ref.1) | copy-start | bytes 3932164
  1.3 86.7 %copy-start.3 = (bf16[8,137,137]{2,0,1:T(8,128)(2,1)S(1)}, bf16[8,137,137]{2,0,1:T(8,128)(2,1)}, u32[]{:S(2)}) copy-start(bf16[8,137,137]{2,0,1:T(8,128)(2,1)} %param.10) | copy-start | bytes 900916
  1.3 86.7 %copy-start.4 = (s32[8,5]{1,0:T(8,128)S(1)}, s32[8,5]{1,0:T(8,128)}, u32[]{:S(2)}) copy-start(s32[8,5]{1,0:T(8,128)} %offsets_ref.1) | copy-start | bytes 484
  1.3 86.7 %copy-start.5 = (f32[8,3]{0,1:T(4,128)S(1)}, f32[8,3]{0,1:T(4,128)}, u32[]{:S(2)}) copy-start(f32[8,3]{0,1:T(4,128)} %param.7) | copy-start | bytes 292
  1.3 86.7 %copy-start.6 = (s32[8]{0:T(128)S(1)}, s32[8]{0:T(128)}, u32[]{:S(2)}) copy-start(s32[8]{0:T(128)} %slots_ref.1) | copy-start | bytes 100
  84.3 3.6 %copy-start = (bf16[4,64,144,128]{3,2,1,0:T(8,128)(2,1)}, bf16[4,64,144,128]{3,2,1,0:T(8,128)(2,1)S(1)}, u32[]{:S(2)}) copy-start(bf16[4,64,144,128]{3,2,1,0:T(8,128)(2,1)S(1)} %gather_rows.1.f_ref) | copy-start | bytes 28311556

commit v2 on v0

v2 whole, which is shorter than its diff:
```python
import functools

import jax
import jax.numpy as jnp
from jax import lax
from jax.experimental import pallas as pl
from jax.experimental.pallas import tpu as pltpu
from jax.sharding import PartitionSpec as P

MESH = pl.DeviceIdType.MESH
SPLIT = 2
LATE = 1


def fused_kernel(
    levels, pad,
    weights_ref, offsets_ref, slots_ref, x_hbm, filters_hbm, vertical_hbm, out_hbm,
    x_ref, filters_ref, vertical_ref, staged, shifted, rows_ref, blended, taps, vert, mixed, done,
    load_sems, send_sems, shift_sems, first_sems, recv_sems, halo_send, halo_recv, ready_sem, store_sems,
):
    o, t = lax.axis_index("lon"), lax.axis_index("lat")
    xh, z = t // 4, t % 4
    xl, y, core = o // 8, (o // 2) % 4, o % 2
    x = 2 * xh + xl
    zp, zm = xh * 4 + (z + 1) % 4, xh * 4 + (z + 3) % 4
    xp = (1 - xh) * 4 + z
    nq = 4 // SPLIT
    per = 2 * SPLIT
    half = 2 * levels * 4

    x_loads = [
        pltpu.make_async_copy(x_hbm.at[pl.ds(k * half, half)], x_ref.at[pl.ds(k * half, half)], load_sems.at[k])
        for k in range(2)
    ]
    weight_loads = [
        pltpu.make_async_copy(filters_hbm, filters_ref, load_sems.at[2]),
        pltpu.make_async_copy(vertical_hbm, vertical_ref, load_sems.at[3]),
    ]
    for load in x_loads:
        load.start()

    ahead = (y + 2 * core) % 4
    shift_to, shift_from = xh * 4 + (z + ahead) % 4, xh * 4 + (z + 4 - ahead) % 4
    stays = ahead == 0
    row_group = (z + 8 - y - 2 * core) % 4
    relay_lat = xl * 4 + z

    def relay_lon(k):
        return xh * 8 + row_group * 2 + k

    def source_lon(j):
        return xh * 8 + ((z + 8 - y - 2 * j) % 4) * 2 + j

    barrier = pltpu.get_barrier_semaphore()

    def greet(lon, lat):
        pl.semaphore_signal(barrier, inc=1, device_id={"lon": lon, "lat": lat}, device_id_type=MESH)

    greet(o, shift_to)
    greet(o, shift_from)
    for k in range(2):
        greet(relay_lon(k), relay_lat)
        greet(source_lon(k), relay_lat)
    for lat in (zp, zm, xp):
        greet(o, lat)
    peers = [(o, xh * 4 + (z + n) % 4) for n in (1, 2, 3)]
    peers += [(xl * 8 + ((y + n) % 4) * 2 + core, t) for n in (1, 2, 3)]
    peers += [(((x + n) % 2) * 8 + y * 2 + core, ((x + n) % 4) // 2 * 4 + z) for n in (1, 2, 3)]
    peers += [(o + 1 - 2 * core, t)]
    for lon, lat in peers:
        greet(lon, lat)

    def each_side(action):
        @pl.when(o > 0)
        def _():
            action(0)

        @pl.when(o < 15)
        def _():
            action(1)

    def crosses(side):
        return o == (8 if side == 0 else 7)

    def greet_side(side):
        greet(o - 1 + 2 * side, t)
        greet(o - 1 + 2 * side, jnp.where(crosses(side), xp, t))

    each_side(greet_side)

    def stage(k):
        for i in (2 * k, 2 * k + 1):
            for q in range(4):
                value = x_ref[pl.ds(i * levels * 4 + q, levels, stride=4), :]
                staged[i, q, 0:levels, :] = value.astype(jnp.bfloat16)
                staged[i, q, levels:pad, :] = jnp.zeros((pad - levels, 128), jnp.bfloat16)

    def shift(k, s, action):
        at = (pl.ds(2 * k, 2), pl.ds(s * nq, nq))
        src, dst = staged.at[at], shifted.at[at]

        @pl.when(stays)
        def _():
            if action == "start":
                pltpu.make_async_copy(src, dst, shift_sems.at[1, k, s]).start()

        @pl.when(jnp.logical_not(stays))
        def _():
            far = pltpu.make_async_remote_copy(
                src, dst, shift_sems.at[0, k, s], shift_sems.at[1, k, s],
                device_id={"lon": o, "lat": shift_to}, device_id_type=MESH,
            )
            if action == "start":
                far.start()
            else:
                far.wait_send()

    def first(k, s, action):
        src = shifted.at[pl.ds(2 * k, 2), pl.ds(s * nq, nq)]
        dst = rows_ref.at[pl.ds(1, 2), pl.ds(4 * o + s * nq, nq)]
        here = recv_sems.at[0, 0, core * SPLIT + s]
        mine = (relay_lat == t) & (relay_lon(k) == o)

        @pl.when(mine)
        def _():
            if action == "start":
                pltpu.make_async_copy(src, dst, here).start()

        @pl.when(jnp.logical_not(mine))
        def _():
            far = pltpu.make_async_remote_copy(
                src, dst, first_sems.at[k, s], here,
                device_id={"lon": relay_lon(k), "lat": relay_lat}, device_id_type=MESH,
            )
            if action == "start":
                far.start()
            else:
                far.wait_send()

    edge = (o == 0).astype(jnp.int32) + (o == 15).astype(jnp.int32)
    x_loads[0].wait()
    stage(0)
    pl.semaphore_wait(barrier, 23 - 2 * edge)
    parts = [(k, s) for s in range(SPLIT) for k in range(2)]
    for s in range(SPLIT):
        shift(0, s, "start")
    x_loads[1].wait()
    stage(1)
    for s in range(SPLIT):
        shift(1, s, "start")
    for load in weight_loads:
        load.start()

    for k, s in parts:
        dst = shifted.at[pl.ds(2 * k, 2), pl.ds(s * nq, nq)]
        pltpu.make_async_copy(dst, dst, shift_sems.at[1, k, s]).wait()
        first(k, s, "start")

    @pl.when(edge > 0)
    def _():
        row = jnp.where(o == 0, 0, 3)

        def fill(q, carry):
            rows_ref[row, q] = jnp.zeros((pad, 128), jnp.bfloat16)
            return carry

        lax.fori_loop(0, 64, fill, 0)

    band = jnp.int32(0)
    for b in range(8):
        band = jnp.where(slots_ref[b] == t, b, band)
    w0, w1, w2 = weights_ref[0, band], weights_ref[1, band], weights_ref[2, band]
    for load in weight_loads:
        load.wait()
    taps[...] = jnp.zeros_like(taps)
    for tap in range(-3, 4):
        total = jnp.zeros((128, 128), jnp.float32)
        for k in range(5):
            hit = (offsets_ref[band, k] == tap).astype(jnp.float32)
            total = total + hit * filters_ref[band, k].astype(jnp.float32)
        block = total.astype(jnp.bfloat16)
        for m in range(2):
            at = tap + 3 + m
            taps[at * 128 : (at + 1) * 128, m * 128 : (m + 1) * 128] = block
    chosen = lax.broadcasted_iota(jnp.int32, (levels, 8, levels), 1) == band
    picked = jnp.sum(jnp.where(chosen, vertical_ref[...].astype(jnp.float32), 0.0), axis=1)
    vert[...] = jnp.zeros_like(vert)
    vert[0:levels, 0:levels] = picked.astype(jnp.bfloat16)

    sends = []

    def block_of(dx, dz, j):
        return ((xh + dx) % 2) * 8 + ((z + dz + 8 - y - 2 * j) % 4) * 2 + j

    def rows_of(dx, dz, n):
        return pl.ds(block_of(dx, dz, n // SPLIT) * 4 + (n % SPLIT) * nq, nq)

    def piece(dx, dz, n):
        return rows_ref.at[pl.ds(1, 2), rows_of(dx, dz, n)]

    def send(dx, dz, n, to, there):
        ref = piece(dx, dz, n)
        copy = pltpu.make_async_remote_copy(
            ref, ref, send_sems.at[len(sends)], recv_sems.at[there[0], there[1], n],
            device_id={"lon": o, "lat": to}, device_id_type=MESH,
        )
        copy.start()
        sends.append(copy)

    def halo(dx, dz, n, side, partner=False):
        q = rows_of(dx, dz, n)
        src = rows_ref.at[1 + side, q]
        dst = rows_ref.at[3 - 3 * side, q]
        slot = block_of(dx, dz, n // SPLIT) * SPLIT + n % SPLIT
        own = block_of(dx + 1, dz, n // SPLIT) * SPLIT + n % SPLIT if partner else slot
        return pltpu.make_async_remote_copy(
            src, dst, halo_send.at[side, own], halo_recv.at[side, slot],
            device_id={"lon": o - 1 + 2 * side, "lat": xp if partner else t}, device_id_type=MESH,
        )

    def start_halo(dx, dz, n, side):
        if dx == 0:
            halo(dx, dz, n, side).start()

            @pl.when(crosses(side))
            def _():
                halo(dx, dz, n, side, True).start()
        else:
            @pl.when(jnp.logical_not(crosses(side)))
            def _():
                halo(dx, dz, n, side).start()

    def arrive(dx, dz, n):
        if (dx, dz) != (0, 0):
            ref = piece(dx, dz, n)
            pltpu.make_async_copy(ref, ref, recv_sems.at[dx, dz, n]).wait()
        late = n % SPLIT >= SPLIT - LATE
        ring = dx == 0 or not late
        if dx == 0 and dz == 0:
            send(dx, dz, n, xp, (1, 0))
        if ring and dz == 0:
            send(dx, dz, n, zp, (dx, 3))
            send(dx, dz, n, zm, (dx, 1))
        if ring and dz == 3 and n < per // 2:
            send(dx, dz, n, zp, (dx, 2))
        if ring and dz == 1 and n >= per // 2:
            send(dx, dz, n, zm, (dx, 2))
        if dx == 0 and dz != 0 and late:
            send(dx, dz, n, xp, (1, dz))
        each_side(lambda side: start_halo(dx, dz, n, side))

    def blend_block(block):
        for s in range(SPLIT):
            for side, present in ((1, o > 0), (0, o < 15)):

                @pl.when(present)
                def _():
                    dst = rows_ref.at[3 - 3 * side, pl.ds(block * 4 + s * nq, nq)]
                    pltpu.make_async_copy(dst, dst, halo_recv.at[side, block * SPLIT + s]).wait()

        for q in range(4):
            rows = [rows_ref[i, block * 4 + q].astype(jnp.float32) for i in range(4)]
            m = (2 * block + (q + 1) // 2) % 32
            for i in range(2):
                value = w0 * rows[i] + w1 * rows[i + 1] + w2 * rows[i + 2]
                blended[i, m, 1 - q % 2] = value.astype(jnp.bfloat16)

    def blend_group(group):
        def body(n, carry):
            blend_block(group * 8 + n)
            return carry

        lax.fori_loop(0, 8, body, 0)

    def store(slot, chunk):
        return pltpu.make_async_copy(
            done.at[slot], out_hbm.at[pl.ds(0, 2), pl.ds(0, levels), pl.ds(pl.multiple_of(chunk * 8, 8), 8)], store_sems.at[slot]
        )

    def chunk_output(chunk, slot):
        for i in range(2):
            blocks = []
            for n in range(7):
                m = (chunk * 4 + n + 31) % 32
                blocks.append(jnp.concatenate([blended[i, m, 0], blended[i, m, 1]], axis=1))
            lhs = jnp.concatenate([jnp.concatenate(blocks[k : k + 4], axis=0) for k in range(4)], axis=1)
            smooth = jnp.dot(lhs, taps[...], preferred_element_type=jnp.float32).astype(jnp.bfloat16)
            wide = jnp.concatenate([smooth[p * pad : (p + 1) * pad] for p in range(4)], axis=1)
            result = jnp.dot(vert[...], wide, preferred_element_type=jnp.float32)
            for n in range(8):
                mixed[pl.ds(n, pad, stride=8), :] = result[:, n * 128 : (n + 1) * 128]
            flat = mixed[0 : levels * 8, :].reshape(levels, 8, 128)
            done[slot, i] = flat.astype(jnp.bfloat16)
        store(slot, chunk).start()

    def outputs(count, first_chunk):
        def body(n, carry):
            chunk = (first_chunk + n) % 8

            @pl.when(n >= 2)
            def _():
                store(n % 2, chunk).wait()

            chunk_output(chunk, n % 2)
            return carry

        lax.fori_loop(0, count, body, 0)
        for slot in range(2):
            store(slot, 0).wait()

    for n in range(per):
        ref = piece(0, 0, n)
        pltpu.make_async_copy(ref, ref, recv_sems.at[0, 0, n]).wait()
    for lon, lat in peers:
        pl.semaphore_signal(ready_sem, inc=1, device_id={"lon": lon, "lat": lat}, device_id_type=MESH)
    pl.semaphore_wait(ready_sem, 10)

    everything = range(per)
    late = [n for n in everything if n % SPLIT >= SPLIT - LATE]
    early = [n for n in everything if n not in late]
    for dx, dz, which in ORDER_1:
        for n in {"all": everything, "late": late, "early": early}[which]:
            arrive(dx, dz, n)
    blend_group(xh)
    outputs(2, 4 * xh + 1)
    for dx, dz, which in ORDER_2:
        for n in {"all": everything, "late": late, "early": early}[which]:
            arrive(dx, dz, n)
    blend_group(1 - xh)
    outputs(6, 4 * xh + 3)

    for k, s in parts:
        shift(k, s, "wait")
        first(k, s, "wait")
    for copy in sends:
        copy.wait_send()
    for dx in range(2):
        for dz in range(4):
            for n in range(per):
                each_side(lambda side: halo(dx, dz, n, side).wait_send())


ORDER_1 = [(0, 0, "all"), (0, 1, "all"), (0, 3, "all"), (1, 0, "all"), (0, 2, "all"), (1, 1, "early"), (1, 3, "early")]
ORDER_2 = [(1, 2, "early"), (1, 1, "late"), (1, 3, "late"), (1, 2, "late")]


def fused(weights, offsets, slots, x, filters, vertical, levels, pad):
    per = 2 * SPLIT
    smem, anywhere = pl.BlockSpec(memory_space=pltpu.SMEM), pl.BlockSpec(memory_space=pl.ANY)
    return pl.pallas_call(
        functools.partial(fused_kernel, levels, pad),
        out_shape=jax.ShapeDtypeStruct((2, levels, 64, 128), jnp.bfloat16),
        in_specs=[smem, smem, smem, anywhere, anywhere, anywhere],
        out_specs=anywhere,
        scratch_shapes=[
            pltpu.VMEM((16 * levels, 128), jnp.float32),
            pltpu.VMEM((8, 5, 128, 128), jnp.bfloat16),
            pltpu.VMEM((levels, 8, levels), jnp.bfloat16),
            pltpu.VMEM((4, 4, pad, 128), jnp.bfloat16),
            pltpu.VMEM((4, 4, pad, 128), jnp.bfloat16),
            pltpu.VMEM((4, 64, pad, 128), jnp.bfloat16),
            pltpu.VMEM((2, 32, 2, pad, 128), jnp.bfloat16),
            pltpu.VMEM((1024, 256), jnp.bfloat16),
            pltpu.VMEM((pad, pad), jnp.bfloat16),
            pltpu.VMEM((pad * 8, 128), jnp.float32),
            pltpu.VMEM((2, 2, levels, 8, 128), jnp.bfloat16),
            pltpu.SemaphoreType.DMA((4,)),
            pltpu.SemaphoreType.DMA((32 * SPLIT,)),
            pltpu.SemaphoreType.DMA((2, 2, SPLIT)),
            pltpu.SemaphoreType.DMA((2, SPLIT)),
            pltpu.SemaphoreType.DMA((2, 4, per)),
            pltpu.SemaphoreType.DMA((2, 8 * per)),
            pltpu.SemaphoreType.DMA((2, 8 * per)),
            pltpu.SemaphoreType.REGULAR,
            pltpu.SemaphoreType.DMA((2,)),
        ],
        compiler_params=pltpu.CompilerParams(
            collective_id=0, has_side_effects=True, vmem_limit_bytes=VMEM_MIB << 20
        ),
        name="fused",
    )(weights, offsets, slots, x, filters, vertical)


VMEM_MIB = 60


def on_device(grad_field, lat_weights, block_offsets, filters, vertical, slot_of_band):
    levels = grad_field.shape[2]
    pad = (levels + 15) // 16 * 16
    x = grad_field.transpose(0, 2, 1, 3).reshape(-1, 128)
    out = fused(
        lat_weights.T, block_offsets, slot_of_band, x, filters, vertical.transpose(1, 0, 2), levels, pad
    )
    return out.transpose(0, 2, 1, 3)[None]


def solution(mesh):
    placed = (P("lat", "lon", None, None), P(), P(), P(), P(), P())
    return jax.shard_map(
        on_device,
        mesh=mesh,
        in_specs=placed,
        out_specs=P("lat", "lon", None, None, None),
        check_vma=False,
    )
```

time: 543 us -> 105 us (0.19)
  the two profiles are of different devices: /device:TPU:2 before, /device:TPU:7 now
where the time goes in v2:
time: 105 us
  Pallas kernels  99.3 us (95%)
  local copies, waits for them, and re-layouts  5.42 us (5%)
    pallas_call x1, Pallas kernels, fused(): pl.pallas_call(functools.partial(fused_kernel, levels, pad), out_shape=ja...  99.3 us
    unnamed x1, local copies, waits for them, and re-layouts  5.42 us

profile of v2, /device:TPU:7, one launch (start us, length us, event | category | flops | bytes accessed | tf_op | source)
XLA Modules:
  0.0 104.8 jit_solution(6769802119906714344)
XLA Ops:
  0.0 99.3 %fused.1 = bf16[2,137,64,128]{3,2,1,0:T(8,128)(2,1)} custom-call(f32[3,8]{1,0:T(4,128)} %bitcast.11, s32[8,5]{1,0:T(8,128)} %offsets_ref.1, s32[8]{0:T(128)} %slots_ref.1, f32[2192,128]{1,0:T(8,128)} %bitcast.9, bf16[8,5,128,128]{3,2,1,0:T(8,128)(2,1)} %filters_hbm.1, bf16[137,8,137]{2,1,0:T(8,128)(2,1)} %bitcast.10), custom_call_target="tpu_custom_call" | custom-call | tf_op jit(solution)/shard_map/fused/pallas_call | solution.py:350
  99.3 5.4 %copy.8 = bf16[1,2,64,137,128]{4,2,3,1,0:T(8,128)(2,1)} copy(bf16[1,2,64,137,128]{4,2,3,1,0:T(8,128)(2,1)} %bitcast.8) | data formatting | bytes 8978432

commit v3 on v2

--- a/solution.py
+++ b/solution.py
@@ -9,14 +9,68 @@
 
 MESH = pl.DeviceIdType.MESH
 SPLIT = 2
-LATE = 1
+LATE = (1,)
+
+
+def chunk_output(chunk, slot, taps, vert, mixed, load_pair, done):
+    levels, pad = done.shape[-3], vert.shape[0]
+    for i in range(2):
+        pairs = [load_pair(i, chunk * 4 + n + 31) for n in range(7)]
+        lhs = jnp.concatenate([jnp.concatenate(pairs[k : k + 4], axis=0) for k in range(4)], axis=1)
+        smooth = jnp.dot(lhs, taps[...], preferred_element_type=jnp.float32).astype(jnp.bfloat16)
+        wide = jnp.concatenate([smooth[p * pad : (p + 1) * pad] for p in range(4)], axis=1)
+        result = jnp.dot(vert[...], wide, preferred_element_type=jnp.float32)
+        for n in range(8):
+            mixed[i, pl.ds(n, pad, stride=8), :] = result[:, n * 128 : (n + 1) * 128]
+        flat = mixed[i, 0 : levels * 8, :].reshape(levels, 8, 128)
+        done[slot, i] = flat.astype(jnp.bfloat16)
+
+
+def outer_kernel(before_ref, here_ref, after_ref, inner_ref, taps_ref, vert_ref, out_ref, mixed):
+    chunk = pl.program_id(0)
+    ready = chunk - 4 * (lax.axis_index("lat") // 4) - 1
+    inner = (ready >= 0) & (ready < 2)
+
+    def load_pair(i, n):
+        ref, m = ((before_ref, 3), *((here_ref, k) for k in range(4)), (after_ref, 0), (after_ref, 1))[n - 31]
+        return jnp.concatenate([ref[i, m, 0], ref[i, m, 1]], axis=1)
+
+    @pl.when(inner)
+    def _():
+        out_ref[...] = inner_ref[...]
+
+    @pl.when(jnp.logical_not(inner))
+    def _():
+        chunk_output(0, 0, taps_ref, vert_ref, mixed, load_pair, out_ref)
+
+
+def outer_outputs(blended, inner, taps, vert, levels, pad):
+    def pairs(shift):
+        return pl.BlockSpec((2, 4, 2, pad, 128), lambda c: (0, (c + shift) % 8, 0, 0, 0))
+
+    return pl.pallas_call(
+        outer_kernel,
+        out_shape=jax.ShapeDtypeStruct((1, 2, levels, 64, 128), jnp.bfloat16),
+        grid=(8,),
+        in_specs=[
+            pairs(7), pairs(0), pairs(1),
+            pl.BlockSpec((1, 2, levels, 8, 128), lambda c: (jnp.clip(c % 4 - 1, 0, 1), 0, 0, 0, 0)),
+            pl.BlockSpec((1024, 256), lambda c: (0, 0)),
+            pl.BlockSpec((pad, pad), lambda c: (0, 0)),
+        ],
+        out_specs=pl.BlockSpec((1, 2, levels, 8, 128), lambda c: (0, 0, 0, c, 0)),
+        scratch_shapes=[pltpu.VMEM((2, pad * 8, 128), jnp.float32)],
+        compiler_params=pltpu.CompilerParams(vmem_limit_bytes=OUTER_MIB << 20),
+        name="outer_outputs",
+    )(blended, blended, blended, inner, taps, vert)
 
 
 def fused_kernel(
     levels, pad,
-    weights_ref, offsets_ref, slots_ref, x_hbm, filters_hbm, vertical_hbm, out_hbm,
+    weights_ref, offsets_ref, slots_ref, x_hbm, filters_hbm, vertical_hbm,
+    blended_hbm, inner_hbm, taps_hbm, vert_hbm,
     x_ref, filters_ref, vertical_ref, staged, shifted, rows_ref, blended, taps, vert, mixed, done,
-    load_sems, send_sems, shift_sems, first_sems, recv_sems, halo_send, halo_recv, ready_sem, store_sems,
+    load_sems, send_sems, shift_sems, first_sems, recv_sems, halo_send, halo_recv, ready_sem, store_sems, out_sems, table_sems,
 ):
     o, t = lax.axis_index("lon"), lax.axis_index("lat")
     xh, z = t // 4, t % 4
@@ -187,6 +241,13 @@
     vert[...] = jnp.zeros_like(vert)
     vert[0:levels, 0:levels] = picked.astype(jnp.bfloat16)
 
+    tables = [
+        pltpu.make_async_copy(taps, taps_hbm, table_sems.at[0]),
+        pltpu.make_async_copy(vert, vert_hbm, table_sems.at[1]),
+    ]
+    for table in tables:
+        table.start()
+
     sends = []
 
     def block_of(dx, dz, j):
@@ -234,7 +295,7 @@
         if (dx, dz) != (0, 0):
             ref = piece(dx, dz, n)
             pltpu.make_async_copy(ref, ref, recv_sems.at[dx, dz, n]).wait()
-        late = n % SPLIT >= SPLIT - LATE
+        late = n in LATE
         ring = dx == 0 or not late
         if dx == 0 and dz == 0:
             send(dx, dz, n, xp, (1, 0))
@@ -265,48 +326,40 @@
                 value = w0 * rows[i] + w1 * rows[i + 1] + w2 * rows[i + 2]
                 blended[i, m, 1 - q % 2] = value.astype(jnp.bfloat16)
 
-    def blend_group(group):
+    def keep(n, count, first):
+        part = pl.ds(0, 2), pl.ds(first, count)
+        return pltpu.make_async_copy(blended.at[part], blended_hbm.at[part], out_sems.at[n])
+
+    def blend_own(n, carry):
+        block = xh * 8 + n
+        blend_block(block)
+
+        @pl.when(n == 0)
+        def _():
+            keep(n, 1, 2 * block + 1).start()
+
+        @pl.when(n > 0)
+        def _():
+            keep(n, 2, 2 * block).start()
+
+        return carry
+
+    def blend_other(n, carry):
+        block = (1 - xh) * 8 + n
+        blend_block(block)
+        keep(8 + n, 2, 2 * block).start()
+        return carry
+
+    def inner_outputs():
         def body(n, carry):
-            blend_block(group * 8 + n)
+            chunk_output(4 * xh + 1 + n, n, taps, vert, mixed, lambda i, m: load_pair(i, m % 32), done)
+            pltpu.make_async_copy(done.at[n], inner_hbm.at[n], store_sems.at[n]).start()
             return carry
 
-        lax.fori_loop(0, 8, body, 0)
-
-    def store(slot, chunk):
-        return pltpu.make_async_copy(
-            done.at[slot], out_hbm.at[pl.ds(0, 2), pl.ds(0, levels), pl.ds(pl.multiple_of(chunk * 8, 8), 8)], store_sems.at[slot]
-        )
-
-    def chunk_output(chunk, slot):
-        for i in range(2):
-            blocks = []
-            for n in range(7):
-                m = (chunk * 4 + n + 31) % 32
-                blocks.append(jnp.concatenate([blended[i, m, 0], blended[i, m, 1]], axis=1))
-            lhs = jnp.concatenate([jnp.concatenate(blocks[k : k + 4], axis=0) for k in range(4)], axis=1)
-            smooth = jnp.dot(lhs, taps[...], preferred_element_type=jnp.float32).astype(jnp.bfloat16)
-            wide = jnp.concatenate([smooth[p * pad : (p + 1) * pad] for p in range(4)], axis=1)
-            result = jnp.dot(vert[...], wide, preferred_element_type=jnp.float32)
-            for n in range(8):
-                mixed[pl.ds(n, pad, stride=8), :] = result[:, n * 128 : (n + 1) * 128]
-            flat = mixed[0 : levels * 8, :].reshape(levels, 8, 128)
-            done[slot, i] = flat.astype(jnp.bfloat16)
-        store(slot, chunk).start()
-
-    def outputs(count, first_chunk):
-        def body(n, carry):
-            chunk = (first_chunk + n) % 8
-
-            @pl.when(n >= 2)
-            def _():
-                store(n % 2, chunk).wait()
-
-            chunk_output(chunk, n % 2)
-            return carry
-
-        lax.fori_loop(0, count, body, 0)
-        for slot in range(2):
-            store(slot, 0).wait()
+        lax.fori_loop(0, 2, body, 0)
+
+    def load_pair(i, m):
+        return jnp.concatenate([blended[i, m, 0], blended[i, m, 1]], axis=1)
 
     for n in range(per):
         ref = piece(0, 0, n)
@@ -316,19 +369,25 @@
     pl.semaphore_wait(ready_sem, 10)
 
     everything = range(per)
-    late = [n for n in everything if n % SPLIT >= SPLIT - LATE]
+    late = [n for n in everything if n in LATE]
     early = [n for n in everything if n not in late]
     for dx, dz, which in ORDER_1:
         for n in {"all": everything, "late": late, "early": early}[which]:
             arrive(dx, dz, n)
-    blend_group(xh)
-    outputs(2, 4 * xh + 1)
+    lax.fori_loop(0, 8, blend_own, 0)
     for dx, dz, which in ORDER_2:
         for n in {"all": everything, "late": late, "early": early}[which]:
             arrive(dx, dz, n)
-    blend_group(1 - xh)
-    outputs(6, 4 * xh + 3)
-
+    inner_outputs()
+    lax.fori_loop(0, 8, blend_other, 0)
+    keep(16, 1, 16 * xh).start()
+
+    for table in tables:
+        table.wait()
+    for n in range(2):
+        pltpu.make_async_copy(done.at[n], inner_hbm.at[n], store_sems.at[n]).wait()
+    for n in range(17):
+        keep(n, 1 if n in (0, 16) else 2, 0).wait()
     for k, s in parts:
         shift(k, s, "wait")
         first(k, s, "wait")
@@ -349,9 +408,14 @@
     smem, anywhere = pl.BlockSpec(memory_space=pltpu.SMEM), pl.BlockSpec(memory_space=pl.ANY)
     return pl.pallas_call(
         functools.partial(fused_kernel, levels, pad),
-        out_shape=jax.ShapeDtypeStruct((2, levels, 64, 128), jnp.bfloat16),
+        out_shape=[
+            jax.ShapeDtypeStruct((2, 32, 2, pad, 128), jnp.bfloat16),
+            jax.ShapeDtypeStruct((2, 2, levels, 8, 128), jnp.bfloat16),
+            jax.ShapeDtypeStruct((1024, 256), jnp.bfloat16),
+            jax.ShapeDtypeStruct((pad, pad), jnp.bfloat16),
+        ],
         in_specs=[smem, smem, smem, anywhere, anywhere, anywhere],
-        out_specs=anywhere,
+        out_specs=[anywhere] * 4,
         scratch_shapes=[
             pltpu.VMEM((16 * levels, 128), jnp.float32),
             pltpu.VMEM((8, 5, 128, 128), jnp.bfloat16),
@@ -362,7 +426,7 @@
             pltpu.VMEM((2, 32, 2, pad, 128), jnp.bfloat16),
             pltpu.VMEM((1024, 256), jnp.bfloat16),
             pltpu.VMEM((pad, pad), jnp.bfloat16),
-            pltpu.VMEM((pad * 8, 128), jnp.float32),
+            pltpu.VMEM((2, pad * 8, 128), jnp.float32),
             pltpu.VMEM((2, 2, levels, 8, 128), jnp.bfloat16),
             pltpu.SemaphoreType.DMA((4,)),
             pltpu.SemaphoreType.DMA((32 * SPLIT,)),
@@ -373,6 +437,8 @@
             pltpu.SemaphoreType.DMA((2, 8 * per)),
             pltpu.SemaphoreType.REGULAR,
             pltpu.SemaphoreType.DMA((2,)),
+            pltpu.SemaphoreType.DMA((17,)),
+            pltpu.SemaphoreType.DMA((2,)),
         ],
         compiler_params=pltpu.CompilerParams(
             collective_id=0, has_side_effects=True, vmem_limit_bytes=VMEM_MIB << 20
@@ -382,16 +448,18 @@
 
 
 VMEM_MIB = 60
+OUTER_MIB = 60
 
 
 def on_device(grad_field, lat_weights, block_offsets, filters, vertical, slot_of_band):
     levels = grad_field.shape[2]
     pad = (levels + 15) // 16 * 16
     x = grad_field.transpose(0, 2, 1, 3).reshape(-1, 128)
-    out = fused(
+    blended, inner, taps, vert = fused(
         lat_weights.T, block_offsets, slot_of_band, x, filters, vertical.transpose(1, 0, 2), levels, pad
     )
-    return out.transpose(0, 2, 1, 3)[None]
+    out = outer_outputs(blended, inner, taps, vert, levels, pad)
+    return out.transpose(0, 1, 3, 2, 4)
 
 
 def solution(mesh):

time: 105 us -> 96.7 us (0.921)
  the two profiles are of different devices: /device:TPU:7 before, /device:TPU:2 now
where the time goes in v3:
time: 96.7 us; the launch traced here: 95.7 us
  Pallas kernels  95.7 us (99%)
    pallas_call x1, Pallas kernels, fused(): pl.pallas_call(functools.partial(fused_kernel, levels, pad), out_shape=[j...  79.6 us
    pallas_call x1, Pallas kernels, outer_outputs(): pl.pallas_call(outer_kernel, out_shape=jax.ShapeDtypeStruct((1, 2, levels...  16 us

profile of v3, /device:TPU:2, one launch (start us, length us, event | category | flops | bytes accessed | tf_op | source)
XLA Modules:
  0.0 95.7 jit_solution(6988352947762605535)
XLA Ops:
  0.0 79.6 %fused.1 = (bf16[2,32,2,144,128]{4,3,2,1,0:T(8,128)(2,1)}, bf16[2,2,137,8,128]{4,3,2,1,0:T(8,128)(2,1)}, bf16[1024,256]{1,0:T(8,128)(2,1)}, bf16[144,144]{1,0:T(8,128)(2,1)}) custom-call(f32[3,8]{1,0:T(4,128)} %bitcast.8, s32[8,5]{1,0:T(8,128)} %offsets_ref.1, s32[8]{0:T(128)} %slots_ref.1, f32[2192,128]{1,0:T(8,128)} %bitcast.6, ...), custom_call_target="tpu_custom_call" | custom-call | tf_op jit(solution)/shard_map/fused/pallas_call | solution.py:409
  79.6 16.0 %outer_outputs.1 = bf16[1,2,137,64,128]{4,3,2,1,0:T(8,128)(2,1)} custom-call(bf16[2,32,2,144,128]{4,3,2,1,0:T(8,128)(2,1)} %get-tuple-element.9.before_ref.here_ref.after_ref, bf16[2,32,2,144,128]{4,3,2,1,0:T(8,128)(2,1)} %get-tuple-element.9.before_ref.here_ref.after_ref, bf16[2,32,2,144,128]{4,3,2,1,0:T(8,128)(2,1)} %get-tuple-element.9.before_ref.here_ref.after_ref, ...), custom_call_target="tpu_custom_call" | custom-call | tf_op jit(solution)/shard_map/outer_outputs/pallas_call | solution.py:51

commit v4 on v3

--- a/solution.py
+++ b/solution.py
@@ -14,55 +14,104 @@
 
 def chunk_output(chunk, slot, taps, vert, mixed, load_pair, done):
     levels, pad = done.shape[-3], vert.shape[0]
+    lhs = []
     for i in range(2):
         pairs = [load_pair(i, chunk * 4 + n + 31) for n in range(7)]
-        lhs = jnp.concatenate([jnp.concatenate(pairs[k : k + 4], axis=0) for k in range(4)], axis=1)
-        smooth = jnp.dot(lhs, taps[...], preferred_element_type=jnp.float32).astype(jnp.bfloat16)
-        wide = jnp.concatenate([smooth[p * pad : (p + 1) * pad] for p in range(4)], axis=1)
-        result = jnp.dot(vert[...], wide, preferred_element_type=jnp.float32)
+        lhs.append(jnp.concatenate([jnp.concatenate(pairs[k : k + 4], axis=0) for k in range(4)], axis=1))
+    lhs = jnp.concatenate(lhs, axis=0)
+    smooth = jnp.dot(lhs, taps[...], preferred_element_type=jnp.float32).astype(jnp.bfloat16)
+    wide = jnp.concatenate([smooth[p * pad : (p + 1) * pad] for p in range(8)], axis=1)
+    result = jnp.dot(vert[...], wide, preferred_element_type=jnp.float32)
+    for i in range(2):
         for n in range(8):
-            mixed[i, pl.ds(n, pad, stride=8), :] = result[:, n * 128 : (n + 1) * 128]
+            at = (8 * i + n) * 128
+            mixed[i, pl.ds(n, pad, stride=8), :] = result[:, at : at + 128]
         flat = mixed[i, 0 : levels * 8, :].reshape(levels, 8, 128)
         done[slot, i] = flat.astype(jnp.bfloat16)
 
 
-def outer_kernel(before_ref, here_ref, after_ref, inner_ref, taps_ref, vert_ref, out_ref, mixed):
-    chunk = pl.program_id(0)
-    ready = chunk - 4 * (lax.axis_index("lat") // 4) - 1
-    inner = (ready >= 0) & (ready < 2)
-
-    def load_pair(i, n):
-        ref, m = ((before_ref, 3), *((here_ref, k) for k in range(4)), (after_ref, 0), (after_ref, 1))[n - 31]
-        return jnp.concatenate([ref[i, m, 0], ref[i, m, 1]], axis=1)
-
-    @pl.when(inner)
-    def _():
-        out_ref[...] = inner_ref[...]
-
-    @pl.when(jnp.logical_not(inner))
-    def _():
-        chunk_output(0, 0, taps_ref, vert_ref, mixed, load_pair, out_ref)
+def outer_kernel(levels, blended_hbm, inner_hbm, taps_hbm, vert_hbm, out_hbm, blended, taps, vert, mixed, done, ready, load_sems, inner_sems, store_sems):
+    xh = lax.axis_index("lat") // 4
+
+    def group(k):
+        part = pl.ds(0, 2), pl.ds(((4 * xh + 2 + k) % 8) * 4, 4)
+        return pltpu.make_async_copy(blended_hbm.at[part], blended.at[part], load_sems.at[k])
+
+    def place(chunk):
+        return out_hbm.at[0, pl.ds(0, 2), pl.ds(0, levels), pl.ds(pl.multiple_of(chunk * 8, 8), 8)]
+
+    def store(slot, chunk):
+        return pltpu.make_async_copy(done.at[slot], place(chunk), store_sems.at[slot])
+
+    tables = [
+        pltpu.make_async_copy(taps_hbm, taps, load_sems.at[8]),
+        pltpu.make_async_copy(vert_hbm, vert, load_sems.at[9]),
+    ]
+    loads = [pltpu.make_async_copy(inner_hbm.at[n], ready.at[n], inner_sems.at[n]) for n in range(2)]
+    inner = [pltpu.make_async_copy(ready.at[n], place(4 * xh + 1 + n), inner_sems.at[2 + n]) for n in range(2)]
+    for k in range(3):
+        group(k).start()
+    for copy in tables:
+        copy.start()
+    for k in range(3, 8):
+        group(k).start()
+    for copy in loads:
+        copy.start()
+    for k in range(2):
+        group(k).wait()
+    for copy in tables:
+        copy.wait()
+
+    def load_pair(i, m):
+        return jnp.concatenate([blended[i, m % 32, 0], blended[i, m % 32, 1]], axis=1)
+
+    def body(n, carry):
+        group(n + 2).wait()
+        chunk = (4 * xh + 3 + n) % 8
+
+        @pl.when(n >= 2)
+        def _():
+            store(n % 2, chunk).wait()
+
+        chunk_output(chunk, n % 2, taps, vert, mixed, load_pair, done)
+        store(n % 2, chunk).start()
+
+        @pl.when(n == 2)
+        def _():
+            for load, copy in zip(loads, inner):
+                load.wait()
+                copy.start()
+
+        return carry
+
+    lax.fori_loop(0, 6, body, 0)
+    for slot in range(2):
+        store(slot, 0).wait()
+    for copy in inner:
+        copy.wait()
 
 
 def outer_outputs(blended, inner, taps, vert, levels, pad):
-    def pairs(shift):
-        return pl.BlockSpec((2, 4, 2, pad, 128), lambda c: (0, (c + shift) % 8, 0, 0, 0))
-
+    anywhere = pl.BlockSpec(memory_space=pl.ANY)
     return pl.pallas_call(
-        outer_kernel,
+        functools.partial(outer_kernel, levels),
         out_shape=jax.ShapeDtypeStruct((1, 2, levels, 64, 128), jnp.bfloat16),
-        grid=(8,),
-        in_specs=[
-            pairs(7), pairs(0), pairs(1),
-            pl.BlockSpec((1, 2, levels, 8, 128), lambda c: (jnp.clip(c % 4 - 1, 0, 1), 0, 0, 0, 0)),
-            pl.BlockSpec((1024, 256), lambda c: (0, 0)),
-            pl.BlockSpec((pad, pad), lambda c: (0, 0)),
+        in_specs=[anywhere] * 4,
+        out_specs=anywhere,
+        scratch_shapes=[
+            pltpu.VMEM((2, 32, 2, pad, 128), jnp.bfloat16),
+            pltpu.VMEM((1024, 256), jnp.bfloat16),
+            pltpu.VMEM((pad, pad), jnp.bfloat16),
+            pltpu.VMEM((2, pad * 8, 128), jnp.float32),
+            pltpu.VMEM((2, 2, levels, 8, 128), jnp.bfloat16),
+            pltpu.VMEM((2, 2, levels, 8, 128), jnp.bfloat16),
+            pltpu.SemaphoreType.DMA((10,)),
+            pltpu.SemaphoreType.DMA((4,)),
+            pltpu.SemaphoreType.DMA((2,)),
         ],
-        out_specs=pl.BlockSpec((1, 2, levels, 8, 128), lambda c: (0, 0, 0, c, 0)),
-        scratch_shapes=[pltpu.VMEM((2, pad * 8, 128), jnp.float32)],
         compiler_params=pltpu.CompilerParams(vmem_limit_bytes=OUTER_MIB << 20),
         name="outer_outputs",
-    )(blended, blended, blended, inner, taps, vert)
+    )(blended, inner, taps, vert)
 
 
 def fused_kernel(
@@ -94,27 +143,35 @@
         load.start()
 
     ahead = (y + 2 * core) % 4
-    shift_to, shift_from = xh * 4 + (z + ahead) % 4, xh * 4 + (z + 4 - ahead) % 4
-    stays = ahead == 0
     row_group = (z + 8 - y - 2 * core) % 4
-    relay_lat = xl * 4 + z
-
-    def relay_lon(k):
-        return xh * 8 + row_group * 2 + k
-
-    def source_lon(j):
-        return xh * 8 + ((z + 8 - y - 2 * j) % 4) * 2 + j
+    swapped = xh * 8 + y * 2 + core
+
+    def shift_to(k):
+        return (swapped, xl * 4 + (z + ahead) % 4) if k == 0 else (o, xh * 4 + (z + ahead) % 4)
+
+    def shift_from(k):
+        return (swapped, xl * 4 + (z + 4 - ahead) % 4) if k == 0 else (o, xh * 4 + (z + 4 - ahead) % 4)
+
+    def stays(k):
+        return (ahead == 0) & (xh == xl) if k == 0 else ahead == 0
+
+    def relay(k):
+        return (xl * 8 + row_group * 2, t) if k == 0 else (xh * 8 + row_group * 2 + 1, xl * 4 + z)
+
+    def source(j):
+        place = ((z + 8 - y - 2 * j) % 4) * 2 + j
+        return jnp.where(core == 0, xl, xh) * 8 + place, jnp.where(core == 0, t, xl * 4 + z)
 
     barrier = pltpu.get_barrier_semaphore()
 
     def greet(lon, lat):
         pl.semaphore_signal(barrier, inc=1, device_id={"lon": lon, "lat": lat}, device_id_type=MESH)
 
-    greet(o, shift_to)
-    greet(o, shift_from)
     for k in range(2):
-        greet(relay_lon(k), relay_lat)
-        greet(source_lon(k), relay_lat)
+        greet(*shift_to(k))
+        greet(*shift_from(k))
+        greet(*relay(k))
+        greet(*source(k))
     for lat in (zp, zm, xp):
         greet(o, lat)
     peers = [(o, xh * 4 + (z + n) % 4) for n in (1, 2, 3)]
@@ -153,16 +210,16 @@
         at = (pl.ds(2 * k, 2), pl.ds(s * nq, nq))
         src, dst = staged.at[at], shifted.at[at]
 
-        @pl.when(stays)
+        @pl.when(stays(k))
         def _():
             if action == "start":
                 pltpu.make_async_copy(src, dst, shift_sems.at[1, k, s]).start()
 
-        @pl.when(jnp.logical_not(stays))
+        @pl.when(jnp.logical_not(stays(k)))
         def _():
             far = pltpu.make_async_remote_copy(
                 src, dst, shift_sems.at[0, k, s], shift_sems.at[1, k, s],
-                device_id={"lon": o, "lat": shift_to}, device_id_type=MESH,
+                device_id={"lon": shift_to(k)[0], "lat": shift_to(k)[1]}, device_id_type=MESH,
             )
             if action == "start":
                 far.start()
@@ -171,9 +228,10 @@
 
     def first(k, s, action):
         src = shifted.at[pl.ds(2 * k, 2), pl.ds(s * nq, nq)]
-        dst = rows_ref.at[pl.ds(1, 2), pl.ds(4 * o + s * nq, nq)]
+        dst = rows_ref.at[pl.ds(1, 2), pl.ds(4 * (swapped if k == 0 else o) + s * nq, nq)]
         here = recv_sems.at[0, 0, core * SPLIT + s]
-        mine = (relay_lat == t) & (relay_lon(k) == o)
+        lon, lat = relay(k)
+        mine = (lat == t) & (lon == o)
 
         @pl.when(mine)
         def _():
@@ -184,7 +242,7 @@
         def _():
             far = pltpu.make_async_remote_copy(
                 src, dst, first_sems.at[k, s], here,
-                device_id={"lon": relay_lon(k), "lat": relay_lat}, device_id_type=MESH,
+                device_id={"lon": lon, "lat": lat}, device_id_type=MESH,
             )
             if action == "start":
                 far.start()
@@ -194,7 +252,7 @@
     edge = (o == 0).astype(jnp.int32) + (o == 15).astype(jnp.int32)
     x_loads[0].wait()
     stage(0)
-    pl.semaphore_wait(barrier, 23 - 2 * edge)
+    pl.semaphore_wait(barrier, 25 - 2 * edge)
     parts = [(k, s) for s in range(SPLIT) for k in range(2)]
     for s in range(SPLIT):
         shift(0, s, "start")

time: 96.7 us -> 86.5 us (0.89)
  Pallas kernels: 95.7 us -> 86 us
    pallas_call x1, Pallas kernels: 16 us -> 9.82 us  [outer_outputs(): pl.pallas_call(functools.partial(outer_kernel, levels), out_shape=jax.Sha...]
    pallas_call x1, Pallas kernels: 79.6 us -> 76.2 us  [fused(): pl.pallas_call(functools.partial(fused_kernel, levels, pad), out_shape=[j...]
where the time goes in v4:
time: 86.5 us; the launch traced here: 86 us
  Pallas kernels  86 us (99%)
    pallas_call x1, Pallas kernels, fused(): pl.pallas_call(functools.partial(fused_kernel, levels, pad), out_shape=[j...  76.2 us
    pallas_call x1, Pallas kernels, outer_outputs(): pl.pallas_call(functools.partial(outer_kernel, levels), out_shape=jax.Sha...  9.82 us

profile of v4, /device:TPU:2, one launch (start us, length us, event | category | flops | bytes accessed | tf_op | source)
XLA Modules:
  0.0 86.0 jit_solution(12623940459005221027)
XLA Ops:
  0.0 76.2 %fused.1 = (bf16[2,32,2,144,128]{4,3,2,1,0:T(8,128)(2,1)}, bf16[2,2,137,8,128]{4,3,2,1,0:T(8,128)(2,1)}, bf16[1024,256]{1,0:T(8,128)(2,1)}, bf16[144,144]{1,0:T(8,128)(2,1)}) custom-call(f32[3,8]{1,0:T(4,128)} %bitcast.8, s32[8,5]{1,0:T(8,128)} %offsets_ref.1, s32[8]{0:T(128)} %slots_ref.1, f32[2192,128]{1,0:T(8,128)} %bitcast.6, ...), custom_call_target="tpu_custom_call" | custom-call | tf_op jit(solution)/shard_map/fused/pallas_call | solution.py:467
  76.2 9.8 %outer_outputs.1 = bf16[1,2,137,64,128]{4,3,2,1,0:T(8,128)(2,1)} custom-call(bf16[2,32,2,144,128]{4,3,2,1,0:T(8,128)(2,1)} %get-tuple-element.9.blended_hbm, bf16[2,2,137,8,128]{4,3,2,1,0:T(8,128)(2,1)} %get-tuple-element.10.inner_hbm, bf16[1024,256]{1,0:T(8,128)(2,1)} %get-tuple-element.11.taps_hbm, bf16[144,144]{1,0:T(8,128)(2,1)} %get-tuple-element.12.vert_hbm), custom_call_target="tpu_custom_call" | custom-call | tf_op jit(solution)/shard_map/outer_outputs/pallas_call | solution.py:96

commit v5 on v4

--- a/solution.py
+++ b/solution.py
@@ -9,7 +9,7 @@
 
 MESH = pl.DeviceIdType.MESH
 SPLIT = 2
-LATE = (1,)
+LATE = (3,)
 
 
 def chunk_output(chunk, slot, taps, vert, mixed, load_pair, done):
@@ -119,7 +119,7 @@
     weights_ref, offsets_ref, slots_ref, x_hbm, filters_hbm, vertical_hbm,
     blended_hbm, inner_hbm, taps_hbm, vert_hbm,
     x_ref, filters_ref, vertical_ref, staged, shifted, rows_ref, blended, taps, vert, mixed, done,
-    load_sems, send_sems, shift_sems, first_sems, recv_sems, halo_send, halo_recv, ready_sem, store_sems, out_sems, table_sems,
+    load_sems, send_sems, shift_sems, first_sems, recv_sems, halo_send, halo_recv, ready_sem, shifted_sem, store_sems, out_sems, table_sems,
 ):
     o, t = lax.axis_index("lon"), lax.axis_index("lat")
     xh, z = t // 4, t % 4
@@ -175,9 +175,7 @@
     for lat in (zp, zm, xp):
         greet(o, lat)
     peers = [(o, xh * 4 + (z + n) % 4) for n in (1, 2, 3)]
-    peers += [(xl * 8 + ((y + n) % 4) * 2 + core, t) for n in (1, 2, 3)]
     peers += [(((x + n) % 2) * 8 + y * 2 + core, ((x + n) % 4) // 2 * 4 + z) for n in (1, 2, 3)]
-    peers += [(o + 1 - 2 * core, t)]
     for lon, lat in peers:
         greet(lon, lat)
 
@@ -252,7 +250,7 @@
     edge = (o == 0).astype(jnp.int32) + (o == 15).astype(jnp.int32)
     x_loads[0].wait()
     stage(0)
-    pl.semaphore_wait(barrier, 25 - 2 * edge)
+    pl.semaphore_wait(barrier, 21 - 2 * edge)
     parts = [(k, s) for s in range(SPLIT) for k in range(2)]
     for s in range(SPLIT):
         shift(0, s, "start")
@@ -267,6 +265,9 @@
         dst = shifted.at[pl.ds(2 * k, 2), pl.ds(s * nq, nq)]
         pltpu.make_async_copy(dst, dst, shift_sems.at[1, k, s]).wait()
         first(k, s, "start")
+
+    for lon, lat in peers[:3]:
+        pl.semaphore_signal(shifted_sem, inc=1, device_id={"lon": lon, "lat": lat}, device_id_type=MESH)
 
     @pl.when(edge > 0)
     def _():
@@ -317,14 +318,17 @@
     def piece(dx, dz, n):
         return rows_ref.at[pl.ds(1, 2), rows_of(dx, dz, n)]
 
-    def send(dx, dz, n, to, there):
+    def send(dx, dz, n, to, there, only=None):
         ref = piece(dx, dz, n)
         copy = pltpu.make_async_remote_copy(
             ref, ref, send_sems.at[len(sends)], recv_sems.at[there[0], there[1], n],
             device_id={"lon": o, "lat": to}, device_id_type=MESH,
         )
-        copy.start()
-        sends.append(copy)
+        sends.append((copy, only))
+        if only is None:
+            copy.start()
+        else:
+            pl.when(only)(copy.start)
 
     def halo(dx, dz, n, side, partner=False):
         q = rows_of(dx, dz, n)
@@ -349,23 +353,28 @@
             def _():
                 halo(dx, dz, n, side).start()
 
+    boundary = ((xl == 0) & (y == 3)) | ((xl == 1) & (y == 0))
+
+    def ring_start(dx, n, only=None):
+        send(dx, 0, n, zp, (dx, 3), only)
+        send(dx, 0, n, zm, (dx, 1), only)
+
     def arrive(dx, dz, n):
         if (dx, dz) != (0, 0):
             ref = piece(dx, dz, n)
             pltpu.make_async_copy(ref, ref, recv_sems.at[dx, dz, n]).wait()
         late = n in LATE
-        ring = dx == 0 or not late
-        if dx == 0 and dz == 0:
+        only = boundary if dx == 1 and late else None
+        if (dx, dz) == (0, 0):
             send(dx, dz, n, xp, (1, 0))
-        if ring and dz == 0:
-            send(dx, dz, n, zp, (dx, 3))
-            send(dx, dz, n, zm, (dx, 1))
-        if ring and dz == 3 and n < per // 2:
-            send(dx, dz, n, zp, (dx, 2))
-        if ring and dz == 1 and n >= per // 2:
-            send(dx, dz, n, zm, (dx, 2))
+        elif dz == 0:
+            ring_start(dx, n, only)
+        if dz == 3 and n < per // 2:
+            send(dx, dz, n, zp, (dx, 2), only)
+        if dz == 1 and n >= per // 2:
+            send(dx, dz, n, zm, (dx, 2), only)
         if dx == 0 and dz != 0 and late:
-            send(dx, dz, n, xp, (1, dz))
+            send(dx, dz, n, xp, (1, dz), jnp.logical_not(boundary))
         each_side(lambda side: start_halo(dx, dz, n, side))
 
     def blend_block(block):
@@ -422,9 +431,12 @@
     for n in range(per):
         ref = piece(0, 0, n)
         pltpu.make_async_copy(ref, ref, recv_sems.at[0, 0, n]).wait()
+        if n == 0:
+            pl.semaphore_wait(shifted_sem, 3)
+        ring_start(0, n)
     for lon, lat in peers:
         pl.semaphore_signal(ready_sem, inc=1, device_id={"lon": lon, "lat": lat}, device_id_type=MESH)
-    pl.semaphore_wait(ready_sem, 10)
+    pl.semaphore_wait(ready_sem, NPEERS)
 
     everything = range(per)
     late = [n for n in everything if n in LATE]
@@ -449,16 +461,19 @@
     for k, s in parts:
         shift(k, s, "wait")
         first(k, s, "wait")
-    for copy in sends:
-        copy.wait_send()
+    for copy, only in sends:
+        if only is None:
+            copy.wait_send()
+        else:
+            pl.when(only)(copy.wait_send)
     for dx in range(2):
         for dz in range(4):
             for n in range(per):
                 each_side(lambda side: halo(dx, dz, n, side).wait_send())
 
 
-ORDER_1 = [(0, 0, "all"), (0, 1, "all"), (0, 3, "all"), (1, 0, "all"), (0, 2, "all"), (1, 1, "early"), (1, 3, "early")]
-ORDER_2 = [(1, 2, "early"), (1, 1, "late"), (1, 3, "late"), (1, 2, "late")]
+ORDER_1 = [(0, 0, "all"), (0, 1, "all"), (0, 3, "all"), (1, 0, "all"), (0, 2, "all"), (1, 1, "all"), (1, 3, "all")]
+ORDER_2 = [(1, 2, "all")]
 
 
 def fused(weights, offsets, slots, x, filters, vertical, levels, pad):
@@ -487,12 +502,13 @@
             pltpu.VMEM((2, pad * 8, 128), jnp.float32),
             pltpu.VMEM((2, 2, levels, 8, 128), jnp.bfloat16),
             pltpu.SemaphoreType.DMA((4,)),
-            pltpu.SemaphoreType.DMA((32 * SPLIT,)),
+            pltpu.SemaphoreType.DMA((48 * SPLIT,)),
             pltpu.SemaphoreType.DMA((2, 2, SPLIT)),
             pltpu.SemaphoreType.DMA((2, SPLIT)),
             pltpu.SemaphoreType.DMA((2, 4, per)),
             pltpu.SemaphoreType.DMA((2, 8 * per)),
             pltpu.SemaphoreType.DMA((2, 8 * per)),
+            pltpu.SemaphoreType.REGULAR,
             pltpu.SemaphoreType.REGULAR,
             pltpu.SemaphoreType.DMA((2,)),
             pltpu.SemaphoreType.DMA((17,)),
@@ -505,6 +521,7 @@
     )(weights, offsets, slots, x, filters, vertical)
 
 
+NPEERS = 6
 VMEM_MIB = 60
 OUTER_MIB = 60
 

time: 86.5 us -> 80.5 us (0.931)
  the two profiles are of different devices: /device:TPU:2 before, /device:TPU:17 now
where the time goes in v5:
time: 80.5 us; the launch traced here: 80.3 us
  Pallas kernels  80.3 us (100%)
    pallas_call x1, Pallas kernels, fused(): pl.pallas_call(functools.partial(fused_kernel, levels, pad), out_shape=[j...  70.5 us
    pallas_call x1, Pallas kernels, outer_outputs(): pl.pallas_call(functools.partial(outer_kernel, levels), out_shape=jax.Sha...  9.82 us

profile of v5, /device:TPU:17, one launch (start us, length us, event | category | flops | bytes accessed | tf_op | source)
XLA Modules:
  0.0 80.3 jit_solution(7400992704982261421)
XLA Ops:
  0.0 70.5 %fused.1 = (bf16[2,32,2,144,128]{4,3,2,1,0:T(8,128)(2,1)}, bf16[2,2,137,8,128]{4,3,2,1,0:T(8,128)(2,1)}, bf16[1024,256]{1,0:T(8,128)(2,1)}, bf16[144,144]{1,0:T(8,128)(2,1)}) custom-call(f32[3,8]{1,0:T(4,128)} %bitcast.8, s32[8,5]{1,0:T(8,128)} %offsets_ref.1, s32[8]{0:T(128)} %slots_ref.1, f32[2192,128]{1,0:T(8,128)} %bitcast.6, ...), custom_call_target="tpu_custom_call" | custom-call | tf_op jit(solution)/shard_map/fused/pallas_call | solution.py:482
  70.5 9.8 %outer_outputs.1 = bf16[1,2,137,64,128]{4,3,2,1,0:T(8,128)(2,1)} custom-call(bf16[2,32,2,144,128]{4,3,2,1,0:T(8,128)(2,1)} %get-tuple-element.9.blended_hbm, bf16[2,2,137,8,128]{4,3,2,1,0:T(8,128)(2,1)} %get-tuple-element.10.inner_hbm, bf16[1024,256]{1,0:T(8,128)(2,1)} %get-tuple-element.11.taps_hbm, bf16[144,144]{1,0:T(8,128)(2,1)} %get-tuple-element.12.vert_hbm), custom_call_target="tpu_custom_call" | custom-call | tf_op jit(solution)/shard_map/outer_outputs/pallas_call | solution.py:96

commit v6 on v5

--- a/solution.py
+++ b/solution.py
@@ -428,27 +428,26 @@
     def load_pair(i, m):
         return jnp.concatenate([blended[i, m, 0], blended[i, m, 1]], axis=1)
 
-    for n in range(per):
+    pl.semaphore_wait(shifted_sem, 3)
+    for n in sorted(range(per), key=lambda n: n % SPLIT):
         ref = piece(0, 0, n)
         pltpu.make_async_copy(ref, ref, recv_sems.at[0, 0, n]).wait()
-        if n == 0:
-            pl.semaphore_wait(shifted_sem, 3)
         ring_start(0, n)
     for lon, lat in peers:
         pl.semaphore_signal(ready_sem, inc=1, device_id={"lon": lon, "lat": lat}, device_id_type=MESH)
     pl.semaphore_wait(ready_sem, NPEERS)
 
-    everything = range(per)
+    everything = sorted(range(per), key=lambda n: n % SPLIT)
     late = [n for n in everything if n in LATE]
     early = [n for n in everything if n not in late]
     for dx, dz, which in ORDER_1:
         for n in {"all": everything, "late": late, "early": early}[which]:
             arrive(dx, dz, n)
     lax.fori_loop(0, 8, blend_own, 0)
+    inner_outputs()
     for dx, dz, which in ORDER_2:
         for n in {"all": everything, "late": late, "early": early}[which]:
             arrive(dx, dz, n)
-    inner_outputs()
     lax.fori_loop(0, 8, blend_other, 0)
     keep(16, 1, 16 * xh).start()
 

time: 80.5 us -> 79.8 us (level)
  the two profiles are of different devices: /device:TPU:17 before, /device:TPU:2 now
where the time goes in v6:
time: 79.8 us; the launch traced here: 78.3 us
  Pallas kernels  78.3 us (98%)
    pallas_call x1, Pallas kernels, fused(): pl.pallas_call(functools.partial(fused_kernel, levels, pad), out_shape=[j...  68.4 us
    pallas_call x1, Pallas kernels, outer_outputs(): pl.pallas_call(functools.partial(outer_kernel, levels), out_shape=jax.Sha...  9.82 us

profile of v6, /device:TPU:2, one launch (start us, length us, event | category | flops | bytes accessed | tf_op | source)
XLA Modules:
  0.0 78.3 jit_solution(17205372718451503189)
XLA Ops:
  0.0 68.4 %fused.1 = (bf16[2,32,2,144,128]{4,3,2,1,0:T(8,128)(2,1)}, bf16[2,2,137,8,128]{4,3,2,1,0:T(8,128)(2,1)}, bf16[1024,256]{1,0:T(8,128)(2,1)}, bf16[144,144]{1,0:T(8,128)(2,1)}) custom-call(f32[3,8]{1,0:T(4,128)} %bitcast.8, s32[8,5]{1,0:T(8,128)} %offsets_ref.1, s32[8]{0:T(128)} %slots_ref.1, f32[2192,128]{1,0:T(8,128)} %bitcast.6, ...), custom_call_target="tpu_custom_call" | custom-call | tf_op jit(solution)/shard_map/fused/pallas_call | solution.py:481
  68.4 9.8 %outer_outputs.1 = bf16[1,2,137,64,128]{4,3,2,1,0:T(8,128)(2,1)} custom-call(bf16[2,32,2,144,128]{4,3,2,1,0:T(8,128)(2,1)} %get-tuple-element.9.blended_hbm, bf16[2,2,137,8,128]{4,3,2,1,0:T(8,128)(2,1)} %get-tuple-element.10.inner_hbm, bf16[1024,256]{1,0:T(8,128)(2,1)} %get-tuple-element.11.taps_hbm, bf16[144,144]{1,0:T(8,128)(2,1)} %get-tuple-element.12.vert_hbm), custom_call_target="tpu_custom_call" | custom-call | tf_op jit(solution)/shard_map/outer_outputs/pallas_call | solution.py:96

commit v7 on v6

--- a/solution.py
+++ b/solution.py
@@ -102,7 +102,7 @@
             pltpu.VMEM((2, 32, 2, pad, 128), jnp.bfloat16),
             pltpu.VMEM((1024, 256), jnp.bfloat16),
             pltpu.VMEM((pad, pad), jnp.bfloat16),
-            pltpu.VMEM((2, pad * 8, 128), jnp.float32),
+            pltpu.VMEM((2, pad * 8 + 8, 128), jnp.float32),
             pltpu.VMEM((2, 2, levels, 8, 128), jnp.bfloat16),
             pltpu.VMEM((2, 2, levels, 8, 128), jnp.bfloat16),
             pltpu.SemaphoreType.DMA((10,)),
@@ -489,7 +489,7 @@
         in_specs=[smem, smem, smem, anywhere, anywhere, anywhere],
         out_specs=[anywhere] * 4,
         scratch_shapes=[
-            pltpu.VMEM((16 * levels, 128), jnp.float32),
+            pltpu.VMEM((16 * levels + 8, 128), jnp.float32),
             pltpu.VMEM((8, 5, 128, 128), jnp.bfloat16),
             pltpu.VMEM((levels, 8, levels), jnp.bfloat16),
             pltpu.VMEM((4, 4, pad, 128), jnp.bfloat16),
@@ -498,7 +498,7 @@
             pltpu.VMEM((2, 32, 2, pad, 128), jnp.bfloat16),
             pltpu.VMEM((1024, 256), jnp.bfloat16),
             pltpu.VMEM((pad, pad), jnp.bfloat16),
-            pltpu.VMEM((2, pad * 8, 128), jnp.float32),
+            pltpu.VMEM((2, pad * 8 + 8, 128), jnp.float32),
             pltpu.VMEM((2, 2, levels, 8, 128), jnp.bfloat16),
             pltpu.SemaphoreType.DMA((4,)),
             pltpu.SemaphoreType.DMA((48 * SPLIT,)),

time: 79.8 us -> 79.8 us (level)
  no operation moved by 1% of the time
where the time goes in v7:
time: 79.8 us; the launch traced here: 78.3 us
  Pallas kernels  78.2 us (98%)
    pallas_call x1, Pallas kernels, fused(): pl.pallas_call(functools.partial(fused_kernel, levels, pad), out_shape=[j...  68.4 us
    pallas_call x1, Pallas kernels, outer_outputs(): pl.pallas_call(functools.partial(outer_kernel, levels), out_shape=jax.Sha...  9.81 us

profile of v7, /device:TPU:2, one launch (start us, length us, event | category | flops | bytes accessed | tf_op | source)
XLA Modules:
  0.0 78.3 jit_solution(9957012894424939949)
XLA Ops:
  0.0 68.4 %fused.1 = (bf16[2,32,2,144,128]{4,3,2,1,0:T(8,128)(2,1)}, bf16[2,2,137,8,128]{4,3,2,1,0:T(8,128)(2,1)}, bf16[1024,256]{1,0:T(8,128)(2,1)}, bf16[144,144]{1,0:T(8,128)(2,1)}) custom-call(f32[3,8]{1,0:T(4,128)} %bitcast.8, s32[8,5]{1,0:T(8,128)} %offsets_ref.1, s32[8]{0:T(128)} %slots_ref.1, f32[2192,128]{1,0:T(8,128)} %bitcast.6, ...), custom_call_target="tpu_custom_call" | custom-call | tf_op jit(solution)/shard_map/fused/pallas_call | solution.py:481
  68.4 9.8 %outer_outputs.1 = bf16[1,2,137,64,128]{4,3,2,1,0:T(8,128)(2,1)} custom-call(bf16[2,32,2,144,128]{4,3,2,1,0:T(8,128)(2,1)} %get-tuple-element.9.blended_hbm, bf16[2,2,137,8,128]{4,3,2,1,0:T(8,128)(2,1)} %get-tuple-element.10.inner_hbm, bf16[1024,256]{1,0:T(8,128)(2,1)} %get-tuple-element.11.taps_hbm, bf16[144,144]{1,0:T(8,128)(2,1)} %get-tuple-element.12.vert_hbm), custom_call_target="tpu_custom_call" | custom-call | tf_op jit(solution)/shard_map/outer_outputs/pallas_call | solution.py:96
